TPU v7x, 32 devices: a whole 2x2x4 slice. The times are simulated.
32 devices in a mesh: block: 8 (over y, x, core), tok: 4 (over z).
Axes of the slice: x: 2, y: 2, z: 4, core: 2. Of those that a mesh axis runs over, the one named last changes fastest.
Arguments:
- queries: bfloat16 [8192, 1536], P(('block', 'tok')), may hold values from -6 to 6
- key_rows: bfloat16 [8192, 1536], P(('block', 'tok')), may hold values from -6 to 6
- value_rows: bfloat16 [8192, 1536], P(('block', 'tok')), may hold values from -6 to 6
- step_rates: float32 [8192, 4], P(('block', 'tok')), may hold values from 0.000637888 to 0.005103104
- fast_in: float32 [8, 4, 3, 384, 384], P('block', None, None, 'tok'), may hold values from -2 to 2
Outputs:
- applied: bfloat16 [8192, 1536], P(('block', 'tok'))
- handed: float32 [8, 4, 3, 384, 384], P('block', None, None, 'tok')
All inputs are finite; a program needn't handle non-finite values.
Results may differ from a plain program's by a relative error of at most 0.03.
Values may be sent and summed in bfloat16 or wider, within the bound.
No kernel may reach another device: no remote copies, remote signals or barrier semaphores. Data moves between devices by JAX's collectives and lax.ppermute only.
A program may use at most 64 MiB of HBM per device.

v0:
```python
import jax
import jax.numpy as jnp
from jax import lax
from jax.sharding import PartitionSpec as P

epsilon = 1e-06


def shifted(block, axis, distance):
    devices = range(lax.axis_size(axis))
    route = [((i - distance) % len(devices), i) for i in devices]
    return lax.ppermute(block, axis, route)


def fast_grads(key_rows, value_rows, step_rates, weights):
    token_count = key_rows.shape[0]
    head_count = weights.shape[0]
    head_width = weights.shape[-1]
    key_heads = key_rows.reshape(token_count, head_count, head_width)
    value_heads = value_rows.reshape(token_count, head_count, head_width)
    gate_pre = jnp.einsum(
        "thi,hij->thj", key_heads, weights[:, 0], preferred_element_type=jnp.float32
    )
    up_pre = jnp.einsum(
        "thi,hij->thj", key_heads, weights[:, 1], preferred_element_type=jnp.float32
    )
    sig_gate = jax.nn.sigmoid(gate_pre)
    activated = gate_pre * sig_gate
    hidden = (activated * up_pre).astype(jnp.bfloat16)
    target = (-(step_rates[:, :, None] * value_heads.astype(jnp.float32))).astype(jnp.bfloat16)
    back_hidden = jnp.einsum(
        "tho,hjo->thj", target, weights[:, 2], preferred_element_type=jnp.float32
    )
    grad_gate = (back_hidden * up_pre * sig_gate * (1.0 + gate_pre * (1.0 - sig_gate))).astype(
        jnp.bfloat16
    )
    grad_up = (back_hidden * activated).astype(jnp.bfloat16)
    first = jnp.einsum("thi,thj->hij", key_heads, grad_gate, preferred_element_type=jnp.float32)
    third = jnp.einsum("thi,thj->hij", key_heads, grad_up, preferred_element_type=jnp.float32)
    second = jnp.einsum("thj,tho->hjo", hidden, target, preferred_element_type=jnp.float32)
    return jnp.stack([first, third, second], axis=1)


def apply_heads(queries, weights):
    token_count = queries.shape[0]
    head_count = weights.shape[0]
    head_width = weights.shape[-1]
    query_heads = queries.reshape(token_count, head_count, head_width)
    gate_pre = jnp.einsum(
        "thi,hij->thj", query_heads, weights[:, 0], preferred_element_type=jnp.float32
    )
    up_pre = jnp.einsum(
        "thi,hij->thj", query_heads, weights[:, 1], preferred_element_type=jnp.float32
    )
    hidden = (jax.nn.silu(gate_pre) * up_pre).astype(jnp.bfloat16)
    result = jnp.einsum("thj,hjo->tho", hidden, weights[:, 2], preferred_element_type=jnp.float32)
    return result.reshape(token_count, head_count * head_width).astype(jnp.bfloat16)


def body(queries, key_rows, value_rows, step_rates, fast_in):
    own_weights = fast_in[0]
    shard_rows = own_weights.shape[2]
    whole_weights = lax.all_gather(
        own_weights.astype(jnp.bfloat16), "tok", axis=2, tiled=True
    ).astype(own_weights.dtype)
    grads = fast_grads(key_rows, value_rows, step_rates, whole_weights.astype(jnp.bfloat16))
    grad_sum = lax.psum(grads.astype(jnp.bfloat16), "tok").astype(jnp.float32)
    stepped = whole_weights - grad_sum
    old_sq = jnp.sum(whole_weights * whole_weights, axis=2)
    new_sq = jnp.sum(stepped * stepped, axis=2)
    renewed_full = stepped * jnp.sqrt((old_sq + epsilon) / (new_sq + epsilon))[:, :, None, :]
    applied = apply_heads(queries, renewed_full.astype(jnp.bfloat16))
    renewed = lax.dynamic_slice_in_dim(
        renewed_full, lax.axis_index("tok") * shard_rows, shard_rows, 2
    )
    handed = shifted(renewed[None].astype(jnp.bfloat16), "block", 1).astype(jnp.float32)
    return (applied, handed)


def solution(mesh):
    return jax.shard_map(
        body,
        mesh=mesh,
        in_specs=(
            P(("block", "tok"), None),
            P(("block", "tok"), None),
            P(("block", "tok"), None),
            P(("block", "tok"), None),
            P("block", None, None, "tok", None),
        ),
        out_specs=(P(("block", "tok"), None), P("block", None, None, "tok", None)),
        check_vma=False,
    )
```

profile of v0, /device:TPU:0, one launch (start us, length us, event | category | flops | bytes accessed | tf_op | source)
XLA Modules:
  0.0 256.2 jit_solution(12328413302557399226)
XLA Ops:
  7.2 0.0 all-gather.3.cloned.1.call-start
  7.2 2.6 copy.64
  9.8 0.0 all-gather.3.cloned.1.call-update
  9.8 0.0 all-reduce.2.cloned.1.call-start
  9.9 0.0 copy-done.7
  9.9 1.3 convert_element_type.74
  11.2 71.4 %all-gather.3.cloned.1.call-done = bf16[1,4,3,384,384]{4,3,1,2,0:T(8,128)(2,1)} async-done(((bf16[1,4,3,96,384]{4,3,1,2,0:T(8,128)(2,1)}), bf16[1,4,3,384,384]{4,3,1,2,0:T(8,128)(2,1)}) %all-gather.3.cloned.1.call-update) | async-done | bytes 3538960 | tf_op jit(solution)/shard_map/all_gather | solution.py:63
  82.6 2.3 fusion.22
  84.9 0.3 copy-done
  85.2 1.9 fusion.21
  87.1 0.7 fusion.23
  87.9 0.0 copy-start.5
  87.9 1.0 fusion.19
  88.9 0.1 copy-done.5
  89.0 0.8 fusion.18
  89.8 1.0 fusion.17
  90.8 2.1 pad_maximum_fusion
  92.9 0.0 all-reduce.2.cloned.1.call-update
  92.9 132.5 %all-reduce.2.cloned.1.call-done = bf16[4,3,384,384]{3,2,0,1:T(8,128)(2,1)} async-done(((bf16[4,3,384,384]{3,2,0,1:T(8,128)(2,1)}), bf16[4,3,384,384]{3,2,0,1:T(8,128)(2,1)}) %all-reduce.2.cloned.1.call-update) | async-done | bytes 3538960 | tf_op jit(solution)/shard_map/psum | solution.py:67
  225.4 3.8 %fusion = (f32[4,3,384]{2,0,1:T(4,128)S(1)}, f32[4,3,384]{2,0,1:T(4,128)S(1)}) fusion(bf16[1,4,3,384,384]{4,3,1,2,0:T(8,128)(2,1)S(1)} %copy-done, bf16[4,3,384,384]{3,2,0,1:T(8,128)(2,1)} %all-reduce.2.cloned.1.call-done), kind=kLoop, calls=%fused_computation.2 | loop fusion | flops 12377088 | bytes 7114752 | tf_op jit(solution)/shard_map/reduce_sum | solution.py:69
  229.3 1.1 fusion.1
  230.4 0.0 copy-start.2
  230.4 1.7 copy-done.2
  232.2 1.0 fusion.24
  233.2 0.0 collective-permute-start
  233.2 0.4 copy-done.6
  233.6 1.2 copy.41
  234.8 3.5 %fusion.20 = f32[4,384,256]{1,2,0:T(8,128)} fusion(bf16[256,4,384]{0,2,1:T(8,128)(2,1)} %bitcast.136, bf16[4,3,384,384]{3,2,0,1:T(8,128)(2,1)} %copy-done.2), kind=kOutput, calls=%fused_computation.42 | convolution fusion | flops 301989888 | bytes 3538944 | tf_op jit(solution)/shard_map/thi,hij->thj/dot_general | solution.py:49
  238.2 3.8 %convolution_convert_fusion.3 = bf16[4,384,256]{2,1,0:T(8,128)(2,1)} fusion(bf16[4,3,384,384]{3,2,0,1:T(8,128)(2,1)S(1)} %copy-done.3, f32[4,384,256]{1,2,0:T(8,128)} %fusion.20, bf16[256,4,384]{0,2,1:T(8,128)(2,1)} %bitcast.137), kind=kOutput, calls=%fused_computation.39 | convolution fusion | flops 606732288 | bytes 5505024 | tf_op jit(solution)/shard_map/thj,hjo->tho/dot_general | solution.py:56
  242.0 2.3 copy.26
  244.3 2.6 %collective-permute-done = bf16[1,4,3,96,384]{4,3,1,2,0:T(8,128)(2,1)} collective-permute-done((bf16[1,4,3,96,384]{4,3,1,2,0:T(8,128)(2,1)}, bf16[1,4,3,96,384]{4,3,1,2,0:T(8,128)(2,1)}, u32[]{:S(2)}, u32[]{:S(2)}) %collective-permute-start) | collective-permute-done | bytes 884768 | tf_op jit(solution)/shard_map/ppermute | solution.py:12
  246.9 2.5 copy.27
  (12 shorter events, 0.0 us)
Async XLA Ops:
  7.2 2.7 %copy-start.7 = (bf16[256,1536]{1,0:T(8,128)(2,1)S(1)}, bf16[256,1536]{1,0:T(8,128)(2,1)}, u32[]{:S(2)}) copy-start(bf16[256,1536]{1,0:T(8,128)(2,1)} %param.7) | copy-start | bytes 2359300
  7.2 75.4 %all-gather.3.cloned.1.call-start = ((), (), s32[]{:S(2)}) async-start(), calls=%async_computation.1 | async-start | bytes 4423680 | tf_op jit(solution)/shard_map/all_gather | solution.py:63
  9.8 215.6 %all-reduce.2.cloned.1.call-start = ((), (), s32[]{:S(2)}) async-start(), calls=%async_computation | async-start | bytes 7077888 | tf_op jit(solution)/shard_map/psum | solution.py:67
  82.6 2.6 %copy-start = (bf16[1,4,3,384,384]{4,3,1,2,0:T(8,128)(2,1)S(1)}, bf16[1,4,3,384,384]{4,3,1,2,0:T(8,128)(2,1)}, u32[]{:S(2)}) copy-start(bf16[1,4,3,384,384]{4,3,1,2,0:T(8,128)(2,1)} %all-gather.3.cloned.1.call-done) | copy-start | bytes 10616836
  85.2 1.9 copy-start.4
  85.2 1.9 copy-start.8
  87.9 1.1 copy-start.5
  225.4 3.9 %copy-start.1 = (bf16[4,3,384,384]{3,2,0,1:T(8,128)(2,1)S(1)}, bf16[4,3,384,384]{3,2,0,1:T(8,128)(2,1)}, u32[]{:S(2)}) copy-start(bf16[4,3,384,384]{3,2,0,1:T(8,128)(2,1)} %all-reduce.2.cloned.1.call-done) | copy-start | bytes 10616836
  230.4 1.8 copy-start.2
  232.2 1.4 copy-start.6
  233.2 13.7 %collective-permute-start = (bf16[1,4,3,96,384]{4,3,1,2,0:T(8,128)(2,1)}, bf16[1,4,3,96,384]{4,3,1,2,0:T(8,128)(2,1)}, u32[]{:S(2)}, u32[]{:S(2)}) collective-permute-start(bf16[1,4,3,96,384]{4,3,1,2,0:T(8,128)(2,1)} %fusion.24), channel_id=1, source_target_pairs={{28,0},{0,4},{4,8},{8,12},{12,16},{16,20},{20,24},{24,28},{29,1},{... | collective-permute-start | bytes 2654216 | tf_op jit(solution)/shard_map/ppermute | solution.py:12
  234.8 3.5 %copy-start.3 = (bf16[4,3,384,384]{3,2,0,1:T(8,128)(2,1)S(1)}, bf16[4,3,384,384]{3,2,0,1:T(8,128)(2,1)}, u32[]{:S(2)}) copy-start(bf16[4,3,384,384]{3,2,0,1:T(8,128)(2,1)} %copy-done.2) | copy-start | bytes 10616836
Sparse Core Ops, SparseCore 0:
  9.9 72.6 all-gather.2
  93.0 132.3 all-reduce.1
where the time goes:
time: 257 us; the launch traced here: 256 us
  waiting for transfers between devices  207 us (81%)
  matrix products  14.9 us (6%)
  between operations  14.2 us (6%)
  local copies, waits for them, and re-layouts  12.2 us (5%)
  other arithmetic  8.38 us (3%)
    psum x1, waiting for transfers between devices, body(): grad_sum = lax.psum(grads.astype(jnp.bfloat16), 'tok').astype(jnp.float32)  133 us
    all_gather x1, waiting for transfers between devices, body(): lax.all_gather(own_weights.astype(jnp.bfloat16), 'tok', axis=2, tiled=True)  71.4 us
    unnamed x21, local copies, waits for them, and re-layouts  9.99 us
  transfers between devices with their start and end apart: 3, of which 3 were waited for; matrix products, arithmetic and copies ran while one was open for 5% of the time, Pallas kernels for 0%

commit v1 on v0

--- a/solution.py
+++ b/solution.py
@@ -1,7 +1,12 @@
+import functools
+
 import jax
 import jax.numpy as jnp
 from jax import lax
+from jax.experimental import pallas as pl
+from jax.experimental.pallas import tpu as pltpu
 from jax.sharding import PartitionSpec as P
+
 
 epsilon = 1e-06
 
@@ -57,7 +62,7 @@
     return result.reshape(token_count, head_count * head_width).astype(jnp.bfloat16)
 
 
-def body(queries, key_rows, value_rows, step_rates, fast_in):
+def gathered_body(queries, key_rows, value_rows, step_rates, fast_in):
     own_weights = fast_in[0]
     shard_rows = own_weights.shape[2]
     whole_weights = lax.all_gather(
@@ -77,6 +82,406 @@
     return (applied, handed)
 
 
+def call(kernel, outs, scratch, place, args, flops=0, kept=(), limit=40):
+    moved = sum(a.size * a.dtype.itemsize for a in (*args, *outs))
+    spec = pl.BlockSpec(memory_space=pltpu.VMEM)
+    far = pl.BlockSpec(memory_space=pltpu.HBM)
+    return pl.pallas_call(
+        kernel,
+        out_shape=outs,
+        in_specs=[pl.BlockSpec(memory_space=pltpu.SMEM)]
+        + [far if i in kept else spec for i in range(len(args))],
+        out_specs=[spec] * len(outs),
+        scratch_shapes=scratch,
+        compiler_params=pltpu.CompilerParams(vmem_limit_bytes=limit << 20),
+        cost_estimate=pl.CostEstimate(flops=flops, bytes_accessed=moved, transcendentals=0),
+    )(place, *args)
+
+
+def rows_dot(a, b):
+    return lax.dot_general(a, b, (((0,), (0,)), ((), ())), preferred_element_type=jnp.float32)
+
+
+def columns_dot(a, b):
+    return lax.dot_general(a, b, (((1,), (1,)), ((), ())), preferred_element_type=jnp.float32)
+
+
+def plain_dot(a, b):
+    return jnp.dot(a, b, preferred_element_type=jnp.float32)
+
+
+LANES = 128
+
+
+def span(start, size, unit):
+    return pl.ds(pl.multiple_of(start, unit), size)
+
+
+class Sizes:
+    def __init__(self, tokens, rows, width):
+        self.tokens, self.rows, self.width = tokens, rows, width
+        self.blocks = width // LANES
+        self.target_at = self.blocks * tokens
+        self.down_at = 2 * self.blocks * tokens
+        self.gate_at = self.down_at + self.blocks * rows
+        self.first_end = self.gate_at + 2 * rows
+        self.late = 2 * (self.blocks - 1) * rows
+        self.query_at = self.first_end + self.late
+        self.mate_end = self.query_at + 2 * self.blocks * tokens
+        self.late_width = width - LANES
+
+
+def pack_kernel(sizes, place_ref, *refs):
+    far, outs, near, sems = refs[:5], refs[5:12], refs[12:17], refs[17]
+    own_ref, mate_ref, cross_ref, cross_late_ref, other_ref, other_late_ref, query_ref = outs
+    copies = [pltpu.make_async_copy(far[i], near[i], sems.at[i]) for i in range(5)]
+    for copy in copies:
+        copy.start()
+    rate_ref, key_ref, value_ref, weight_ref, queries_ref = near
+    tokens, rows, width, blocks = sizes.tokens, sizes.rows, sizes.width, sizes.blocks
+    here = place_ref[0]
+    parts = (
+        (here ^ 1, mate_ref, (mate_ref, sizes.first_end)),
+        (here ^ 3, cross_ref, (cross_late_ref, 0)),
+        (here ^ 2, other_ref, (other_late_ref, 0)),
+        (here, own_ref, (own_ref, sizes.first_end)),
+    )
+    copies[0].wait()
+    copies[1].wait()
+    for head, message, _ in parts:
+        for c in range(blocks):
+            at = span(head * width + c * LANES, LANES, LANES)
+            message[c * tokens : (c + 1) * tokens] = key_ref[:, at]
+    rates = rate_ref[...]
+    row = lax.broadcasted_iota(jnp.int32, rates.shape, 0)
+    copies[2].wait()
+    for head, message, _ in parts:
+        rate = jnp.sum(jnp.where(row == head, rates, 0.0), axis=0, keepdims=True)
+        rate = jnp.broadcast_to(rate, (LANES, tokens)).T
+        for c in range(blocks):
+            at = span(head * width + c * LANES, LANES, LANES)
+            start = sizes.target_at + c * tokens
+            value = value_ref[:, at].astype(jnp.float32)
+            message[start : start + tokens] = (-(rate * value)).astype(jnp.bfloat16)
+    copies[3].wait()
+    for head, message, (late, late_at) in parts:
+        for m in range(2):
+            start = sizes.gate_at + m * rows
+            message[start : start + rows] = weight_ref[head, m, :, :LANES].astype(jnp.bfloat16)
+            for c in range(1, blocks):
+                start = late_at + (m * (blocks - 1) + c - 1) * rows
+                late[start : start + rows] = weight_ref[
+                    head, m, :, c * LANES : (c + 1) * LANES
+                ].astype(jnp.bfloat16)
+        for c in range(blocks):
+            start = sizes.down_at + c * rows
+            message[start : start + rows] = weight_ref[
+                head, 2, :, c * LANES : (c + 1) * LANES
+            ].astype(jnp.bfloat16)
+    copies[4].wait()
+    for i, head in enumerate((here ^ 1, here ^ 3)):
+        for c in range(blocks):
+            at = span(head * width + c * LANES, LANES, LANES)
+            start = sizes.query_at + (i * blocks + c) * tokens
+            mate_ref[start : start + tokens] = queries_ref[:, at]
+    for i, head in enumerate((here, here ^ 2)):
+        query_ref[i] = queries_ref[:, span(head * width, width, LANES)]
+
+
+def pre_grads(pre, back, half):
+    gate_pre, up_pre = pre[:, :half], pre[:, half:]
+    sig_gate = jax.nn.sigmoid(gate_pre)
+    activated = gate_pre * sig_gate
+    hidden = (activated * up_pre).astype(jnp.bfloat16)
+    gate = (back * up_pre * sig_gate * (1.0 + gate_pre * (1.0 - sig_gate))).astype(jnp.bfloat16)
+    return hidden, gate, (back * activated).astype(jnp.bfloat16)
+
+
+def renewal(old, grad):
+    old = old.astype(jnp.float32)
+    stepped = old - grad
+    old_sq = jnp.sum(old * old, axis=0, keepdims=True)
+    new_sq = jnp.sum(stepped * stepped, axis=0, keepdims=True)
+    return (stepped * jnp.sqrt((old_sq + epsilon) / (new_sq + epsilon))).astype(jnp.bfloat16)
+
+
+def quarters(here):
+    return (here, here ^ 1, here ^ 3, here ^ 2)
+
+
+def first_kernel(sizes, place_ref, *refs):
+    messages = refs[:4]
+    keys, targets, down, hidden_ref, first_ref, weights, gates = refs[4:]
+    tokens, rows, blocks = sizes.tokens, sizes.rows, sizes.blocks
+    for g, (source, message) in enumerate(zip(quarters(place_ref[0]), messages)):
+        at = span(source * rows, rows, 16)
+        mine = slice(g * tokens, (g + 1) * tokens)
+        for m in range(2):
+            start = sizes.gate_at + m * rows
+            weights[at, m * LANES : (m + 1) * LANES] = message[start : start + rows]
+        for c in range(blocks):
+            lanes = slice(c * LANES, (c + 1) * LANES)
+            keys[mine, lanes] = message[c * tokens : (c + 1) * tokens]
+            start = sizes.target_at + c * tokens
+            targets[mine, lanes] = message[start : start + tokens]
+            start = sizes.down_at + c * rows
+            down[at, lanes] = message[start : start + rows]
+    for g in range(4):
+        mine = slice(g * tokens, (g + 1) * tokens)
+        pre = plain_dot(keys[mine], weights[...])
+        back = columns_dot(targets[mine], down[:LANES])
+        hidden_ref[mine], gates[mine, :LANES], gates[mine, LANES:] = pre_grads(pre, back, LANES)
+    first_ref[...] = renewal(weights[...], rows_dot(keys[...], gates[...]))
+
+
+def second_kernel(sizes, place_ref, *refs):
+    keys, targets, down, early, first, own, mate, cross, other = refs[:9]
+    late_ref, down_ref, near_ref, far0_ref, far1_ref, same_ref, mate_ref = refs[9:16]
+    weights, gates, hidden = refs[16:]
+    tokens, rows, blocks, late = sizes.tokens, sizes.rows, sizes.blocks, sizes.late_width
+    here = place_ref[0]
+    starts = (sizes.first_end, sizes.first_end, 0, 0)
+    for source, message, start in zip(quarters(here), (own, mate, cross, other), starts):
+        at = span(source * rows, rows, 16)
+        for i in range(2 * (blocks - 1)):
+            weights[at, i * LANES : (i + 1) * LANES] = message[
+                start + i * rows : start + (i + 1) * rows
+            ]
+    hidden[:, :LANES] = early[...]
+    for g in range(4):
+        mine = slice(g * tokens, (g + 1) * tokens)
+        pre = plain_dot(keys[mine], weights[...])
+        back = columns_dot(targets[mine], down[LANES:])
+        hidden[mine, LANES:], gates[mine, :late], gates[mine, late:] = pre_grads(pre, back, late)
+    late_ref[...] = renewal(weights[...], rows_dot(keys[...], gates[...]))
+    down_ref[...] = renewal(down[...], rows_dot(hidden[...], targets[...]))
+    half = lax.shift_right_logical(here, 1)
+    near_ref[...] = down_ref[span((1 - half) * 2 * rows, 2 * rows, 16)]
+    far = span(half * 2 * rows, 2 * rows, 16)
+    far0_ref[...] = down_ref[far, :late]
+    far1_ref[...] = down_ref[far, late:]
+    for ref, row in ((same_ref, here), (mate_ref, here ^ 1)):
+        at = span(row * rows, rows, 16)
+        hand_rows(ref, at, first, late_ref, late)
+        ref[2] = down_ref[at]
+
+
+def hand_rows(ref, at, first, second, late):
+    for m in range(2):
+        ref[m, :, :LANES] = first[at, m * LANES : (m + 1) * LANES]
+        ref[m, :, LANES:] = second[at, m * late : (m + 1) * late]
+
+
+def hidden_of(query, first, second, late):
+    pre, pre_late = plain_dot(query, first[...]), plain_dot(query, second[...])
+    gate, up = pre[:, :LANES], pre[:, LANES:]
+    gate_late, up_late = pre_late[:, :late], pre_late[:, late:]
+    return (
+        (gate * jax.nn.sigmoid(gate) * up).astype(jnp.bfloat16),
+        (gate_late * jax.nn.sigmoid(gate_late) * up_late).astype(jnp.bfloat16),
+    )
+
+
+def mate_query(sizes, mate, i):
+    tokens, blocks = sizes.tokens, sizes.blocks
+    start = sizes.query_at + i * blocks * tokens
+    return jnp.concatenate(
+        [mate[start + c * tokens : start + (c + 1) * tokens] for c in range(blocks)], axis=1
+    )
+
+
+def own_kernel(sizes, place_ref, query, mate, first, second, down, own_ref, mate_ref):
+    late = sizes.late_width
+    for tokens, ref in ((mate_query(sizes, mate, 0), mate_ref), (query[0], own_ref)):
+        early, after = hidden_of(tokens, first, second, late)
+        result = plain_dot(early, down[:LANES]) + plain_dot(after, down[LANES:])
+        ref[...] = result.astype(jnp.bfloat16)
+
+
+def other_kernel(sizes, place_ref, *refs):
+    query, mate, first, second, near = refs[:5]
+    hidden_ref, same_ref, mate_ref = refs[5:]
+    late, rows, tokens = sizes.late_width, sizes.rows, sizes.tokens
+    here = place_ref[0]
+    for ref, row in ((mate_ref, here ^ 1), (same_ref, here)):
+        hand_rows(ref, span(row * rows, rows, 16), first, second, late)
+        ref[2] = near[span((row & 1) * rows, rows, 16)]
+    for g, q in enumerate((mate_query(sizes, mate, 1), query[1])):
+        mine = slice(g * tokens, (g + 1) * tokens)
+        hidden_ref[mine, :LANES], hidden_ref[mine, LANES:] = hidden_of(q, first, second, late)
+
+
+def result_kernel(sizes, start, place_ref, hidden, near, far, own_ref, mate_ref, down):
+    half = lax.shift_right_logical(place_ref[0], 1)
+    rows, tokens, columns = 2 * sizes.rows, sizes.tokens, far.shape[-1]
+    down[span(half * rows, rows, 16)] = near[:, start : start + columns]
+    down[span((1 - half) * rows, rows, 16)] = far[...]
+    mate_ref[...] = plain_dot(hidden[:tokens], down[...]).astype(jnp.bfloat16)
+    own_ref[...] = plain_dot(hidden[tokens:], down[...]).astype(jnp.bfloat16)
+
+
+def handed_kernel(place_ref, *refs):
+    here = place_ref[0]
+    for head, ref in zip((here, here ^ 1, here ^ 2, here ^ 3), refs[:4]):
+        refs[4][0, head] = ref[...].astype(jnp.float32)
+
+
+def applied_kernel(sizes, place_ref, own, mate, own0, own1, mate0, mate1, applied_ref):
+    here, width, late = place_ref[0], sizes.width, sizes.late_width
+    applied_ref[:, span(here * width, width, LANES)] = own[...]
+    applied_ref[:, span((here ^ 1) * width, width, LANES)] = mate[...]
+    for head, (first, second) in ((here ^ 2, (own0, own1)), (here ^ 3, (mate0, mate1))):
+        applied_ref[:, span(head * width, late, LANES)] = first[...]
+        applied_ref[:, span(head * width + late, LANES, LANES)] = second[...]
+
+
+def head_body(queries, key_rows, value_rows, step_rates, fast_in):
+    _, heads, matrices, rows, width = fast_in.shape
+    tokens = queries.shape[0]
+    blocks = lax.axis_size("block")
+    place = lax.axis_index("tok").astype(jnp.int32)[None]
+    sizes = Sizes(tokens, rows, width)
+    late = sizes.late_width
+    flops = 2 * tokens * width * width
+
+    def bf16(*shape):
+        return jax.ShapeDtypeStruct(shape, jnp.bfloat16)
+
+    def swapped(value, mask):
+        return lax.ppermute(value, "tok", [(i, i ^ mask) for i in range(heads)])
+
+    def next_block(value, mask):
+        route = [
+            (b * heads + z, ((b + 1) % blocks) * heads + (z ^ mask))
+            for b in range(blocks)
+            for z in range(heads)
+        ]
+        return lax.ppermute(value, ("block", "tok"), route)
+
+    arrays = (step_rates.T, key_rows, value_rows, fast_in[0], queries)
+    own, mate, cross, cross_late, other, other_late, query = call(
+        functools.partial(pack_kernel, sizes),
+        [
+            bf16(sizes.query_at, LANES),
+            bf16(sizes.mate_end, LANES),
+            bf16(sizes.first_end, LANES),
+            bf16(sizes.late, LANES),
+            bf16(sizes.first_end, LANES),
+            bf16(sizes.late, LANES),
+            bf16(2, tokens, width),
+        ],
+        [pltpu.VMEM(a.shape, a.dtype) for a in arrays] + [pltpu.SemaphoreType.DMA((5,))],
+        place,
+        arrays,
+        kept=range(5),
+        limit=40,
+    )
+    mate = swapped(mate, 1)
+    cross = swapped(cross, 3)
+    other = swapped(other, 2)
+    cross_late = swapped(cross_late, 3)
+    other_late = swapped(other_late, 2)
+
+    keys, targets, down, early, first = call(
+        functools.partial(first_kernel, sizes),
+        [
+            bf16(heads * tokens, width),
+            bf16(heads * tokens, width),
+            bf16(width, width),
+            bf16(heads * tokens, LANES),
+            bf16(width, 2 * LANES),
+        ],
+        [
+            pltpu.VMEM((width, 2 * LANES), jnp.bfloat16),
+            pltpu.VMEM((heads * tokens, 2 * LANES), jnp.bfloat16),
+        ],
+        place,
+        (own, mate, cross, other),
+        6 * heads * flops // 3,
+    )
+    first_in = swapped(first, 2)
+    second, down, near, far0, far1, same_rows, mate_rows = call(
+        functools.partial(second_kernel, sizes),
+        [
+            bf16(width, 2 * late),
+            bf16(width, width),
+            bf16(2 * rows, width),
+            bf16(2 * rows, late),
+            bf16(2 * rows, LANES),
+            bf16(matrices, rows, width),
+            bf16(matrices, rows, width),
+        ],
+        [
+            pltpu.VMEM((width, 2 * late), jnp.bfloat16),
+            pltpu.VMEM((heads * tokens, 2 * late), jnp.bfloat16),
+            pltpu.VMEM((heads * tokens, width), jnp.bfloat16),
+        ],
+        place,
+        (keys, targets, down, early, first, own, mate, cross_late, other_late),
+        12 * heads * flops // 3,
+    )
+    second_in = swapped(second, 2)
+    near_in = swapped(near, 2)
+    far0_in = swapped(far0, 2)
+    far1_in = swapped(far1, 2)
+    own_result, mate_result = call(
+        functools.partial(own_kernel, sizes),
+        [bf16(tokens, width)] * 2,
+        [],
+        place,
+        (query, mate, first, second, down),
+        6 * flops,
+    )
+    mate_result = swapped(mate_result, 1)
+    handed_own = next_block(same_rows, 0)
+    handed_mate = next_block(mate_rows, 1)
+
+    hidden, same_rows, mate_rows = call(
+        functools.partial(other_kernel, sizes),
+        [bf16(2 * tokens, width), bf16(matrices, rows, width), bf16(matrices, rows, width)],
+        [],
+        place,
+        (query, mate, first_in, second_in, near_in),
+        4 * flops,
+    )
+    handed_cross = next_block(mate_rows, 1)
+    handed_other = next_block(same_rows, 0)
+    own_parts, mate_parts = [], []
+    for i, far in enumerate((far0_in, far1_in)):
+        columns = far.shape[-1]
+        own_part, mate_part = call(
+            functools.partial(result_kernel, sizes, i * late),
+            [bf16(tokens, columns)] * 2,
+            [pltpu.VMEM((width, columns), jnp.bfloat16)],
+            place,
+            (hidden, near_in, far),
+            2 * flops * columns // width,
+        )
+        own_parts.append(own_part)
+        mate_parts.append(swapped(mate_part, 1))
+    (handed,) = call(
+        handed_kernel,
+        [jax.ShapeDtypeStruct((1, heads, matrices, rows, width), jnp.float32)],
+        [],
+        place,
+        (handed_own, handed_mate, handed_other, handed_cross),
+    )
+    (applied,) = call(
+        functools.partial(applied_kernel, sizes),
+        [bf16(tokens, heads * width)],
+        [],
+        place,
+        (own_result, mate_result, *own_parts, *mate_parts),
+    )
+    return (applied, handed)
+
+
+def body(queries, key_rows, value_rows, step_rates, fast_in):
+    by_head = fast_in.shape[1] == lax.axis_size("tok") == 4
+    chosen = head_body if by_head else gathered_body
+    return chosen(queries, key_rows, value_rows, step_rates, fast_in)
+
+
 def solution(mesh):
     return jax.shard_map(
         body,

time: 257 us -> 128 us (0.50)
  waiting for transfers between devices: 207 us -> 89.4 us
  starting transfers between devices: 0.08 us -> 22.9 us
  matrix products: 14.9 us -> 0 us
  between operations: 14.2 us -> 0.76 us
  Pallas kernels: 0 us -> 9.2 us
  other arithmetic: 8.38 us -> 0 us
  local copies, waits for them, and re-layouts: 12.2 us -> 5.55 us
    psum x1 -> x0, waiting for transfers between devices: 133 us -> none  [body(): grad_sum = lax.psum(grads.astype(jnp.bfloat16), 'tok').astype(jnp.float32)]
    ppermute x1 -> x17, waiting for transfers between devices: 2.56 us -> 89.4 us  [the longest x13 89.4 us: swapped(): return lax.ppermute(value, 'tok', [(i, i ^ mask) for i in range(heads)])]
    all_gather x1 -> x0, waiting for transfers between devices: 71.4 us -> none  [body(): lax.all_gather(own_weights.astype(jnp.bfloat16), 'tok', axis=2, tiled=True)]
    ppermute x1 -> x17, starting transfers between devices: 0.01 us -> 22.9 us  [the longest x13 19.3 us: swapped(): return lax.ppermute(value, 'tok', [(i, i ^ mask) for i in range(heads)])]
    dot_general x8 -> x0, matrix products: 14.9 us -> none  [the longest x1 3.76 us: apply_heads(): jnp.einsum('thj,hjo->tho', hidden, weights[:, 2], preferred_element_type=...]
    pallas_call x0 -> x9, Pallas kernels: none -> 9.2 us  [call(): pl.pallas_call(kernel, out_shape=outs, in_specs=[pl.BlockSpec(memory_spac...]
    unnamed x21 -> x10, local copies, waits for them, and re-layouts: 9.99 us -> 5.55 us
    reduce_sum x1 -> x0, other arithmetic: 3.81 us -> none  [body(): old_sq = jnp.sum(whole_weights * whole_weights, axis=2)]
  transfers between devices with their start and end apart: 3 -> 17, of which waited for: 3 -> 7; matrix products, arithmetic and copies ran while one was open for 5% -> 0% of each run, Pallas kernels for 0% -> 3%
where the time goes in v1:
time: 128 us
  waiting for transfers between devices  89.4 us (70%)
  starting transfers between devices  22.9 us (18%)
  Pallas kernels  9.2 us (7%)
  local copies, waits for them, and re-layouts  5.55 us (4%)
    ppermute x13, waiting for transfers between devices, swapped(): return lax.ppermute(value, 'tok', [(i, i ^ mask) for i in range(heads)])  89.4 us
    ppermute x13, starting transfers between devices, swapped(): return lax.ppermute(value, 'tok', [(i, i ^ mask) for i in range(heads)])  19.3 us
    pallas_call x9, Pallas kernels, call(): pl.pallas_call(kernel, out_shape=outs, in_specs=[pl.BlockSpec(memory_spac...  9.2 us
    unnamed x10, local copies, waits for them, and re-layouts  5.55 us
    ppermute x4, starting transfers between devices, next_block(): return lax.ppermute(value, ('block', 'tok'), route)  3.51 us
  transfers between devices with their start and end apart: 17, of which 7 were waited for; matrix products, arithmetic and copies ran while one was open for 0% of the time, Pallas kernels for 3%

profile of v1, /device:TPU:0, one launch (start us, length us, event | category | flops | bytes accessed | tf_op | source)
XLA Modules:
  0.0 127.8 jit_solution(17164173252682980422)
XLA Ops:
  0.6 1.5 %copy-done = f32[1,4,3,96,384]{4,3,2,1,0:T(8,128)S(1)} copy-done((f32[1,4,3,96,384]{4,3,2,1,0:T(8,128)S(1)}, f32[1,4,3,96,384]{4,3,2,1,0:T(8,128)}, u32[]{:S(2)}) %copy-start) | copy-done | bytes 1769496
  2.1 1.1 copy-done.1
  3.2 1.1 copy-done.2
  4.4 1.1 copy-done.3
  5.5 0.7 copy-done.4
  6.2 1.1 shard_map.68
  7.3 3.1 %collective-permute-start = (bf16[3936,128]{1,0:T(8,128)(2,1)S(1)}, bf16[3936,128]{1,0:T(8,128)(2,1)S(1)}, u32[]{:S(2)}, u32[]{:S(2)}) collective-permute-start(bf16[3936,128]{1,0:T(8,128)(2,1)S(1)} %get-tuple-element.31), channel_id=1, source_target_pairs={{0,1},{1,0},{2,3},{3,2},{4,5},{5,4},{6,7},{7,6},{8,9},{9,8},{10,11... | collective-permute-start | bytes 3022856 | tf_op jit(solution)/shard_map/ppermute | solution.py:351
  10.5 2.5 %collective-permute-start.1 = (bf16[2016,128]{1,0:T(8,128)(2,1)S(1)}, bf16[2016,128]{1,0:T(8,128)(2,1)S(1)}, u32[]{:S(2)}, u32[]{:S(2)}) collective-permute-start(bf16[2016,128]{1,0:T(8,128)(2,1)S(1)} %get-tuple-element.33), channel_id=1, source_target_pairs={{0,3},{1,2},{2,1},{3,0},{4,7},{5,6},{6,5},{7,4},{8,11},{9,10},{10,... | collective-permute-start | bytes 1548296 | tf_op jit(solution)/shard_map/ppermute | solution.py:351
  13.1 2.9 %collective-permute-start.3 = (bf16[384,128]{1,0:T(8,128)(2,1)S(1)}, bf16[384,128]{1,0:T(8,128)(2,1)S(1)}, u32[]{:S(2)}, u32[]{:S(2)}) collective-permute-start(bf16[384,128]{1,0:T(8,128)(2,1)S(1)} %get-tuple-element.40), channel_id=1, source_target_pairs={{0,3},{1,2},{2,1},{3,0},{4,7},{5,6},{6,5},{7,4},{8,11},{9,10},{10,... | collective-permute-start | bytes 294920 | tf_op jit(solution)/shard_map/ppermute | solution.py:351
  16.0 0.3 collective-permute-start.4
  16.3 30.9 %collective-permute-done.1.refs_2_ = bf16[2016,128]{1,0:T(8,128)(2,1)S(1)} collective-permute-done((bf16[2016,128]{1,0:T(8,128)(2,1)S(1)}, bf16[2016,128]{1,0:T(8,128)(2,1)S(1)}, u32[]{:S(2)}, u32[]{:S(2)}) %collective-permute-start.1) | collective-permute-done | bytes 516128 | tf_op jit(solution)/shard_map/ppermute | solution.py:351
  47.2 15.9 %collective-permute-done.2.refs_3_ = bf16[2016,128]{1,0:T(8,128)(2,1)S(1)} collective-permute-done((bf16[2016,128]{1,0:T(8,128)(2,1)S(1)}, bf16[2016,128]{1,0:T(8,128)(2,1)S(1)}, u32[]{:S(2)}, u32[]{:S(2)}) %collective-permute-start.2) | collective-permute-done | bytes 516128 | tf_op jit(solution)/shard_map/ppermute | solution.py:351
  63.1 1.2 shard_map.69
  64.3 1.9 %collective-permute-done.4.refs_8_ = bf16[384,128]{1,0:T(8,128)(2,1)S(1)} collective-permute-done((bf16[384,128]{1,0:T(8,128)(2,1)S(1)}, bf16[384,128]{1,0:T(8,128)(2,1)S(1)}, u32[]{:S(2)}, u32[]{:S(2)}) %collective-permute-start.4) | collective-permute-done | bytes 98336 | tf_op jit(solution)/shard_map/ppermute | solution.py:351
  66.2 2.3 %shard_map.70 = (bf16[384,512]{1,0:T(8,128)(2,1)S(1)}, bf16[384,384]{1,0:T(8,128)(2,1)S(1)}, bf16[192,384]{1,0:T(8,128)(2,1)S(1)}, bf16[192,256]{1,0:T(8,128)(2,...) custom-call(s32[1]{0:T(128)} %bitcast.place_ref, ...), custom_call_target="tpu_custom_call" | custom-call | flops 1207959552 | bytes 5570560 | tf_op jit(solution)/shard_map/pallas_call | solution.py:89
  68.5 0.8 collective-permute-start.7
  69.2 2.2 %collective-permute-start.6 = (bf16[384,256]{1,0:T(8,128)(2,1)S(1)}, bf16[384,256]{1,0:T(8,128)(2,1)S(1)}, u32[]{:S(2)}, u32[]{:S(2)}) collective-permute-start(bf16[384,256]{1,0:T(8,128)(2,1)S(1)} %get-tuple-element.35.refs_4_.first), channel_id=1, source_target_pairs={{0,2},{1,3},{2,0},{3,1},{4,6},{5,7},{6,4},{7,5},{8,10},{9,11},{10,... | collective-permute-start | bytes 589832 | tf_op jit(solution)/shard_map/ppermute | solution.py:351
  71.5 0.7 collective-permute-start.8
  72.1 1.1 shard_map.71
  73.3 2.6 %collective-permute-start.5 = (bf16[256,384]{1,0:T(8,128)(2,1)S(1)}, bf16[256,384]{1,0:T(8,128)(2,1)S(1)}, u32[]{:S(2)}, u32[]{:S(2)}) collective-permute-start(bf16[256,384]{1,0:T(8,128)(2,1)S(1)} %get-tuple-element.45), channel_id=1, source_target_pairs={{0,1},{1,0},{2,3},{3,2},{4,5},{5,4},{6,7},{7,6},{8,9},{9,8},{10,11... | collective-permute-start | bytes 589832 | tf_op jit(solution)/shard_map/ppermute | solution.py:351
  75.9 28.3 %collective-permute-done.8.refs_4_.near = bf16[192,384]{1,0:T(8,128)(2,1)S(1)} collective-permute-done((bf16[192,384]{1,0:T(8,128)(2,1)S(1)}, bf16[192,384]{1,0:T(8,128)(2,1)S(1)}, u32[]{:S(2)}, u32[]{:S(2)}) %collective-permute-start.8) | collective-permute-done | bytes 147488 | tf_op jit(solution)/shard_map/ppermute | solution.py:351
  104.2 3.2 %collective-permute-start.14 = (bf16[3,96,384]{2,1,0:T(8,128)(2,1)S(1)}, bf16[3,96,384]{2,1,0:T(8,128)(2,1)S(1)}, u32[]{:S(2)}, u32[]{:S(2)}) collective-permute-start(bf16[3,96,384]{2,1,0:T(8,128)(2,1)S(1)} %get-tuple-element.55), channel_id=1, source_target_pairs={{0,5},{1,4},{2,7},{3,6},{4,9},{5,8},{6,11},{7,10},{8,13},{9,12},{1... | collective-permute-start | bytes 663560 | tf_op jit(solution)/shard_map/ppermute | solution.py:359
  107.5 0.6 shard_map.72
  108.1 1.2 collective-permute-done.10.far
  109.3 0.3 collective-permute-start.16
  109.8 3.0 %collective-permute-start.12 = (bf16[256,128]{1,0:T(8,128)(2,1)S(1)}, bf16[256,128]{1,0:T(8,128)(2,1)S(1)}, u32[]{:S(2)}, u32[]{:S(2)}) collective-permute-start(bf16[256,128]{1,0:T(8,128)(2,1)S(1)} %get-tuple-element.53), channel_id=1, source_target_pairs={{0,1},{1,0},{2,3},{3,2},{4,5},{5,4},{6,7},{7,6},{8,9},{9,8},{10,11... | collective-permute-start | bytes 196616 | tf_op jit(solution)/shard_map/ppermute | solution.py:351
  112.9 0.3 shard_map.73
  113.2 6.9 %collective-permute-done.12.mate1 = bf16[256,128]{1,0:T(8,128)(2,1)S(1)} collective-permute-done((bf16[256,128]{1,0:T(8,128)(2,1)S(1)}, bf16[256,128]{1,0:T(8,128)(2,1)S(1)}, u32[]{:S(2)}, u32[]{:S(2)}) %collective-permute-start.12) | collective-permute-done | bytes 65568 | tf_op jit(solution)/shard_map/ppermute | solution.py:351
  120.1 1.0 collective-permute-start.11
  121.1 4.4 %collective-permute-done.11.mate0 = bf16[256,256]{1,0:T(8,128)(2,1)S(1)} collective-permute-done((bf16[256,256]{1,0:T(8,128)(2,1)S(1)}, bf16[256,256]{1,0:T(8,128)(2,1)S(1)}, u32[]{:S(2)}, u32[]{:S(2)}) %collective-permute-start.11) | collective-permute-done | bytes 131104 | tf_op jit(solution)/shard_map/ppermute | solution.py:351
  125.5 1.0 shard_map.75
  126.5 1.3 %shard_map.76 = f32[1,4,3,96,384]{4,3,2,1,0:T(8,128)} custom-call(s32[1]{0:T(128)} %bitcast.place_ref, bf16[3,96,384]{2,1,0:T(8,128)(2,1)S(1)} %collective-permute-done.13.refs_0_, bf16[3,96,384]{2,1,0:T(8,128)(2,1)S(1)} %collective-permute-done.14.refs_1_, bf16[3,96,384]{2,1,0:T(8,128)(2,1)S(1)} %collective-permute-done.15.refs_2_, ...), custom_call_target="tpu_custom_call" | custom-call | bytes 2654208 | tf_op jit(solution)/shard_map/pallas_call | solution.py:89
  (21 shorter events, 0.5 us)
Async XLA Ops:
  0.6 1.5 %copy-start = (f32[1,4,3,96,384]{4,3,2,1,0:T(8,128)S(1)}, f32[1,4,3,96,384]{4,3,2,1,0:T(8,128)}, u32[]{:S(2)}) copy-start(f32[1,4,3,96,384]{4,3,2,1,0:T(8,128)} %param.9) | copy-start | bytes 5308420
  2.1 1.1 copy-start.1
  3.2 1.1 copy-start.2
  4.4 1.1 copy-start.3
  5.5 0.7 copy-start.4
  7.3 55.7 %collective-permute-start = (bf16[3936,128]{1,0:T(8,128)(2,1)S(1)}, bf16[3936,128]{1,0:T(8,128)(2,1)S(1)}, u32[]{:S(2)}, u32[]{:S(2)}) collective-permute-start(bf16[3936,128]{1,0:T(8,128)(2,1)S(1)} %get-tuple-element.31), channel_id=1, source_target_pairs={{0,1},{1,0},{2,3},{3,2},{4,5},{5,4},{6,7},{7,6},{8,9},{9,8},{10,11... | collective-permute-start | bytes 3022856 | tf_op jit(solution)/shard_map/ppermute | solution.py:351
  10.5 36.8 %collective-permute-start.1 = (bf16[2016,128]{1,0:T(8,128)(2,1)S(1)}, bf16[2016,128]{1,0:T(8,128)(2,1)S(1)}, u32[]{:S(2)}, u32[]{:S(2)}) collective-permute-start(bf16[2016,128]{1,0:T(8,128)(2,1)S(1)} %get-tuple-element.33), channel_id=1, source_target_pairs={{0,3},{1,2},{2,1},{3,0},{4,7},{5,6},{6,5},{7,4},{8,11},{9,10},{10,... | collective-permute-start | bytes 1548296 | tf_op jit(solution)/shard_map/ppermute | solution.py:351
  12.9 50.1 %collective-permute-start.2 = (bf16[2016,128]{1,0:T(8,128)(2,1)S(1)}, bf16[2016,128]{1,0:T(8,128)(2,1)S(1)}, u32[]{:S(2)}, u32[]{:S(2)}) collective-permute-start(bf16[2016,128]{1,0:T(8,128)(2,1)S(1)} %get-tuple-element.34), channel_id=1, source_target_pairs={{0,2},{1,3},{2,0},{3,1},{4,6},{5,7},{6,4},{7,5},{8,10},{9,11},{10,... | collective-permute-start | bytes 1548296 | tf_op jit(solution)/shard_map/ppermute | solution.py:351
  13.1 51.2 %collective-permute-start.3 = (bf16[384,128]{1,0:T(8,128)(2,1)S(1)}, bf16[384,128]{1,0:T(8,128)(2,1)S(1)}, u32[]{:S(2)}, u32[]{:S(2)}) collective-permute-start(bf16[384,128]{1,0:T(8,128)(2,1)S(1)} %get-tuple-element.40), channel_id=1, source_target_pairs={{0,3},{1,2},{2,1},{3,0},{4,7},{5,6},{6,5},{7,4},{8,11},{9,10},{10,... | collective-permute-start | bytes 294920 | tf_op jit(solution)/shard_map/ppermute | solution.py:351
  16.0 50.2 %collective-permute-start.4 = (bf16[384,128]{1,0:T(8,128)(2,1)S(1)}, bf16[384,128]{1,0:T(8,128)(2,1)S(1)}, u32[]{:S(2)}, u32[]{:S(2)}) collective-permute-start(bf16[384,128]{1,0:T(8,128)(2,1)S(1)} %get-tuple-element.41), channel_id=1, source_target_pairs={{0,2},{1,3},{2,0},{3,1},{4,6},{5,7},{6,4},{7,5},{8,10},{9,11},{10,... | collective-permute-start | bytes 294920 | tf_op jit(solution)/shard_map/ppermute | solution.py:351
  68.5 35.8 %collective-permute-start.7 = (bf16[384,512]{1,0:T(8,128)(2,1)S(1)}, bf16[384,512]{1,0:T(8,128)(2,1)S(1)}, u32[]{:S(2)}, u32[]{:S(2)}) collective-permute-start(bf16[384,512]{1,0:T(8,128)(2,1)S(1)} %get-tuple-element.42.second), channel_id=1, source_target_pairs={{0,2},{1,3},{2,0},{3,1},{4,6},{5,7},{6,4},{7,5},{8,10},{9,11},{10,... | collective-permute-start | bytes 1179656 | tf_op jit(solution)/shard_map/ppermute | solution.py:351
  69.2 35.0 %collective-permute-start.6 = (bf16[384,256]{1,0:T(8,128)(2,1)S(1)}, bf16[384,256]{1,0:T(8,128)(2,1)S(1)}, u32[]{:S(2)}, u32[]{:S(2)}) collective-permute-start(bf16[384,256]{1,0:T(8,128)(2,1)S(1)} %get-tuple-element.35.refs_4_.first), channel_id=1, source_target_pairs={{0,2},{1,3},{2,0},{3,1},{4,6},{5,7},{6,4},{7,5},{8,10},{9,11},{10,... | collective-permute-start | bytes 589832 | tf_op jit(solution)/shard_map/ppermute | solution.py:351
  71.5 32.8 %collective-permute-start.8 = (bf16[192,384]{1,0:T(8,128)(2,1)S(1)}, bf16[192,384]{1,0:T(8,128)(2,1)S(1)}, u32[]{:S(2)}, u32[]{:S(2)}) collective-permute-start(bf16[192,384]{1,0:T(8,128)(2,1)S(1)} %get-tuple-element.46), channel_id=1, source_target_pairs={{0,2},{1,3},{2,0},{3,1},{4,6},{5,7},{6,4},{7,5},{8,10},{9,11},{10,... | collective-permute-start | bytes 442376 | tf_op jit(solution)/shard_map/ppermute | solution.py:351
  73.3 36.5 %collective-permute-start.5 = (bf16[256,384]{1,0:T(8,128)(2,1)S(1)}, bf16[256,384]{1,0:T(8,128)(2,1)S(1)}, u32[]{:S(2)}, u32[]{:S(2)}) collective-permute-start(bf16[256,384]{1,0:T(8,128)(2,1)S(1)} %get-tuple-element.45), channel_id=1, source_target_pairs={{0,1},{1,0},{2,3},{3,2},{4,5},{5,4},{6,7},{7,6},{8,9},{9,8},{10,11... | collective-permute-start | bytes 589832 | tf_op jit(solution)/shard_map/ppermute | solution.py:351
  75.8 33.4 %collective-permute-start.9 = (bf16[192,256]{1,0:T(8,128)(2,1)S(1)}, bf16[192,256]{1,0:T(8,128)(2,1)S(1)}, u32[]{:S(2)}, u32[]{:S(2)}) collective-permute-start(bf16[192,256]{1,0:T(8,128)(2,1)S(1)} %get-tuple-element.48), channel_id=1, source_target_pairs={{0,2},{1,3},{2,0},{3,1},{4,6},{5,7},{6,4},{7,5},{8,10},{9,11},{10,... | collective-permute-start | bytes 294920 | tf_op jit(solution)/shard_map/ppermute | solution.py:351
  104.2 5.0 %collective-permute-start.10 = (bf16[192,128]{1,0:T(8,128)(2,1)S(1)}, bf16[192,128]{1,0:T(8,128)(2,1)S(1)}, u32[]{:S(2)}, u32[]{:S(2)}) collective-permute-start(bf16[192,128]{1,0:T(8,128)(2,1)S(1)} %get-tuple-element.50), channel_id=1, source_target_pairs={{0,2},{1,3},{2,0},{3,1},{4,6},{5,7},{6,4},{7,5},{8,10},{9,11},{10,... | collective-permute-start | bytes 147464 | tf_op jit(solution)/shard_map/ppermute | solution.py:351
  104.2 22.2 %collective-permute-start.13 = (bf16[3,96,384]{2,1,0:T(8,128)(2,1)S(1)}, bf16[3,96,384]{2,1,0:T(8,128)(2,1)S(1)}, u32[]{:S(2)}, u32[]{:S(2)}) collective-permute-start(bf16[3,96,384]{2,1,0:T(8,128)(2,1)S(1)} %get-tuple-element.54), channel_id=1, source_target_pairs={{0,4},{1,5},{2,6},{3,7},{4,8},{5,9},{6,10},{7,11},{8,12},{9,13},{1... | collective-permute-start | bytes 663560 | tf_op jit(solution)/shard_map/ppermute | solution.py:359
  104.2 22.2 %collective-permute-start.14 = (bf16[3,96,384]{2,1,0:T(8,128)(2,1)S(1)}, bf16[3,96,384]{2,1,0:T(8,128)(2,1)S(1)}, u32[]{:S(2)}, u32[]{:S(2)}) collective-permute-start(bf16[3,96,384]{2,1,0:T(8,128)(2,1)S(1)} %get-tuple-element.55), channel_id=1, source_target_pairs={{0,5},{1,4},{2,7},{3,6},{4,9},{5,8},{6,11},{7,10},{8,13},{9,12},{1... | collective-permute-start | bytes 663560 | tf_op jit(solution)/shard_map/ppermute | solution.py:359
  109.3 17.2 %collective-permute-start.15 = (bf16[3,96,384]{2,1,0:T(8,128)(2,1)S(1)}, bf16[3,96,384]{2,1,0:T(8,128)(2,1)S(1)}, u32[]{:S(2)}, u32[]{:S(2)}) collective-permute-start(bf16[3,96,384]{2,1,0:T(8,128)(2,1)S(1)} %get-tuple-element.56), channel_id=1, source_target_pairs={{0,4},{1,5},{2,6},{3,7},{4,8},{5,9},{6,10},{7,11},{8,12},{9,13},{1... | collective-permute-start | bytes 663560 | tf_op jit(solution)/shard_map/ppermute | solution.py:359
  109.3 17.2 %collective-permute-start.16 = (bf16[3,96,384]{2,1,0:T(8,128)(2,1)S(1)}, bf16[3,96,384]{2,1,0:T(8,128)(2,1)S(1)}, u32[]{:S(2)}, u32[]{:S(2)}) collective-permute-start(bf16[3,96,384]{2,1,0:T(8,128)(2,1)S(1)} %get-tuple-element.57), channel_id=1, source_target_pairs={{0,5},{1,4},{2,7},{3,6},{4,9},{5,8},{6,11},{7,10},{8,13},{9,12},{1... | collective-permute-start | bytes 663560 | tf_op jit(solution)/shard_map/ppermute | solution.py:359
  109.8 10.3 %collective-permute-start.12 = (bf16[256,128]{1,0:T(8,128)(2,1)S(1)}, bf16[256,128]{1,0:T(8,128)(2,1)S(1)}, u32[]{:S(2)}, u32[]{:S(2)}) collective-permute-start(bf16[256,128]{1,0:T(8,128)(2,1)S(1)} %get-tuple-element.53), channel_id=1, source_target_pairs={{0,1},{1,0},{2,3},{3,2},{4,5},{5,4},{6,7},{7,6},{8,9},{9,8},{10,11... | collective-permute-start | bytes 196616 | tf_op jit(solution)/shard_map/ppermute | solution.py:351
  120.1 5.4 %collective-permute-start.11 = (bf16[256,256]{1,0:T(8,128)(2,1)S(1)}, bf16[256,256]{1,0:T(8,128)(2,1)S(1)}, u32[]{:S(2)}, u32[]{:S(2)}) collective-permute-start(bf16[256,256]{1,0:T(8,128)(2,1)S(1)} %get-tuple-element.52), channel_id=1, source_target_pairs={{0,1},{1,0},{2,3},{3,2},{4,5},{5,4},{6,7},{7,6},{8,9},{9,8},{10,11... | collective-permute-start | bytes 393224 | tf_op jit(solution)/shard_map/ppermute | solution.py:351

commit v2 on v1

--- a/solution.py
+++ b/solution.py
@@ -86,7 +86,7 @@
     moved = sum(a.size * a.dtype.itemsize for a in (*args, *outs))
     spec = pl.BlockSpec(memory_space=pltpu.VMEM)
     far = pl.BlockSpec(memory_space=pltpu.HBM)
-    return pl.pallas_call(
+    run = pl.pallas_call(
         kernel,
         out_shape=outs,
         in_specs=[pl.BlockSpec(memory_space=pltpu.SMEM)]
@@ -95,7 +95,12 @@
         scratch_shapes=scratch,
         compiler_params=pltpu.CompilerParams(vmem_limit_bytes=limit << 20),
         cost_estimate=pl.CostEstimate(flops=flops, bytes_accessed=moved, transcendentals=0),
-    )(place, *args)
+    )
+    args = [
+        pltpu.with_memory_space_constraint(a, pltpu.HBM) if i in kept else a
+        for i, a in enumerate(args)
+    ]
+    return run(place, *args)
 
 
 def rows_dot(a, b):
@@ -236,8 +241,8 @@
 
 def second_kernel(sizes, place_ref, *refs):
     keys, targets, down, early, first, own, mate, cross, other = refs[:9]
-    late_ref, down_ref, near_ref, far0_ref, far1_ref, same_ref, mate_ref = refs[9:16]
-    weights, gates, hidden = refs[16:]
+    late_ref, down_ref, near_ref, far_ref, far0_ref, far1_ref, same_ref, mate_ref = refs[9:17]
+    weights, gates, hidden = refs[17:]
     tokens, rows, blocks, late = sizes.tokens, sizes.rows, sizes.blocks, sizes.late_width
     here = place_ref[0]
     starts = (sizes.first_end, sizes.first_end, 0, 0)
@@ -256,8 +261,11 @@
     late_ref[...] = renewal(weights[...], rows_dot(keys[...], gates[...]))
     down_ref[...] = renewal(down[...], rows_dot(hidden[...], targets[...]))
     half = lax.shift_right_logical(here, 1)
-    near_ref[...] = down_ref[span((1 - half) * 2 * rows, 2 * rows, 16)]
+    near = span((1 - half) * 2 * rows, 2 * rows, 16)
     far = span(half * 2 * rows, 2 * rows, 16)
+    near_ref[:, : 2 * late] = late_ref[near]
+    near_ref[:, 2 * late :] = down_ref[near]
+    far_ref[...] = late_ref[far]
     far0_ref[...] = down_ref[far, :late]
     far1_ref[...] = down_ref[far, late:]
     for ref, row in ((same_ref, here), (mate_ref, here ^ 1)):
@@ -298,24 +306,38 @@
         ref[...] = result.astype(jnp.bfloat16)
 
 
-def other_kernel(sizes, place_ref, *refs):
-    query, mate, first, second, near = refs[:5]
-    hidden_ref, same_ref, mate_ref = refs[5:]
-    late, rows, tokens = sizes.late_width, sizes.rows, sizes.tokens
-    here = place_ref[0]
+def rows_kernel(sizes, place_ref, first, near, same_ref, mate_ref):
+    late, rows, here = sizes.late_width, sizes.rows, place_ref[0]
     for ref, row in ((mate_ref, here ^ 1), (same_ref, here)):
-        hand_rows(ref, span(row * rows, rows, 16), first, second, late)
-        ref[2] = near[span((row & 1) * rows, rows, 16)]
+        at = span(row * rows, rows, 16)
+        arrived = span((row & 1) * rows, rows, 16)
+        for m in range(2):
+            ref[m, :, :LANES] = first[at, m * LANES : (m + 1) * LANES]
+            ref[m, :, LANES:] = near[arrived, m * late : (m + 1) * late]
+        ref[2] = near[arrived, 2 * late :]
+
+
+def halves(sizes, here):
+    half, rows = lax.shift_right_logical(here, 1), 2 * sizes.rows
+    return span(half * rows, rows, 16), span((1 - half) * rows, rows, 16)
+
+
+def other_kernel(sizes, place_ref, query, mate, first, near, far, hidden_ref, second):
+    late, tokens = sizes.late_width, sizes.tokens
+    near_at, far_at = halves(sizes, place_ref[0])
+    second[near_at] = near[:, : 2 * late]
+    second[far_at] = far[...]
     for g, q in enumerate((mate_query(sizes, mate, 1), query[1])):
         mine = slice(g * tokens, (g + 1) * tokens)
         hidden_ref[mine, :LANES], hidden_ref[mine, LANES:] = hidden_of(q, first, second, late)
 
 
 def result_kernel(sizes, start, place_ref, hidden, near, far, own_ref, mate_ref, down):
-    half = lax.shift_right_logical(place_ref[0], 1)
-    rows, tokens, columns = 2 * sizes.rows, sizes.tokens, far.shape[-1]
-    down[span(half * rows, rows, 16)] = near[:, start : start + columns]
-    down[span((1 - half) * rows, rows, 16)] = far[...]
+    tokens, columns = sizes.tokens, far.shape[-1]
+    start += 2 * sizes.late_width
+    near_at, far_at = halves(sizes, place_ref[0])
+    down[near_at] = near[:, start : start + columns]
+    down[far_at] = far[...]
     mate_ref[...] = plain_dot(hidden[:tokens], down[...]).astype(jnp.bfloat16)
     own_ref[...] = plain_dot(hidden[tokens:], down[...]).astype(jnp.bfloat16)
 
@@ -400,12 +422,13 @@
         6 * heads * flops // 3,
     )
     first_in = swapped(first, 2)
-    second, down, near, far0, far1, same_rows, mate_rows = call(
+    second, down, near, far, far0, far1, same_rows, mate_rows = call(
         functools.partial(second_kernel, sizes),
         [
             bf16(width, 2 * late),
             bf16(width, width),
-            bf16(2 * rows, width),
+            bf16(2 * rows, 2 * late + width),
+            bf16(2 * rows, 2 * late),
             bf16(2 * rows, late),
             bf16(2 * rows, LANES),
             bf16(matrices, rows, width),
@@ -420,8 +443,8 @@
         (keys, targets, down, early, first, own, mate, cross_late, other_late),
         12 * heads * flops // 3,
     )
-    second_in = swapped(second, 2)
     near_in = swapped(near, 2)
+    far_in = swapped(far, 2)
     far0_in = swapped(far0, 2)
     far1_in = swapped(far1, 2)
     own_result, mate_result = call(
@@ -436,16 +459,23 @@
     handed_own = next_block(same_rows, 0)
     handed_mate = next_block(mate_rows, 1)
 
-    hidden, same_rows, mate_rows = call(
-        functools.partial(other_kernel, sizes),
-        [bf16(2 * tokens, width), bf16(matrices, rows, width), bf16(matrices, rows, width)],
+    same_rows, mate_rows = call(
+        functools.partial(rows_kernel, sizes),
+        [bf16(matrices, rows, width)] * 2,
         [],
         place,
-        (query, mate, first_in, second_in, near_in),
-        4 * flops,
+        (first_in, near_in),
     )
     handed_cross = next_block(mate_rows, 1)
     handed_other = next_block(same_rows, 0)
+    (hidden,) = call(
+        functools.partial(other_kernel, sizes),
+        [bf16(2 * tokens, width)],
+        [pltpu.VMEM((width, 2 * late), jnp.bfloat16)],
+        place,
+        (query, mate, first_in, near_in, far_in),
+        4 * flops,
+    )
     own_parts, mate_parts = [], []
     for i, far in enumerate((far0_in, far1_in)):
         columns = far.shape[-1]

time: 128 us -> 126 us (0.984)
  waiting for transfers between devices: 89.4 us -> 95.6 us
  local copies, waits for them, and re-layouts: 5.55 us -> 0 us
  starting transfers between devices: 22.9 us -> 19.1 us
    ppermute x13, waiting for transfers between devices: 89.4 us -> 95.5 us  [swapped(): return lax.ppermute(value, 'tok', [(i, i ^ mask) for i in range(heads)])]
    unnamed x10 -> x0, local copies, waits for them, and re-layouts: 5.55 us -> none
    ppermute x13, starting transfers between devices: 19.3 us -> 16.2 us  [swapped(): return lax.ppermute(value, 'tok', [(i, i ^ mask) for i in range(heads)])]
    pallas_call x9 -> x10, Pallas kernels: 9.2 us -> 10.4 us  [call(): return run(place, *args)]
  transfers between devices with their start and end apart: 17 -> 17, of which waited for: 7 -> 7; matrix products, arithmetic and copies ran while one was open for 0% -> 0% of each run, Pallas kernels for 3% -> 4%
where the time goes in v2:
time: 126 us
  waiting for transfers between devices  95.6 us (76%)
  starting transfers between devices  19.1 us (15%)
  Pallas kernels  10.4 us (8%)
    ppermute x13, waiting for transfers between devices, swapped(): return lax.ppermute(value, 'tok', [(i, i ^ mask) for i in range(heads)])  95.5 us
    ppermute x13, starting transfers between devices, swapped(): return lax.ppermute(value, 'tok', [(i, i ^ mask) for i in range(heads)])  16.2 us
    pallas_call x10, Pallas kernels, call(): return run(place, *args)  10.4 us
    ppermute x4, starting transfers between devices, next_block(): return lax.ppermute(value, ('block', 'tok'), route)  2.86 us
  transfers between devices with their start and end apart: 17, of which 7 were waited for; matrix products, arithmetic and copies ran while one was open for 0% of the time, Pallas kernels for 4%

profile of v2, /device:TPU:0, one launch (start us, length us, event | category | flops | bytes accessed | tf_op | source)
XLA Modules:
  0.0 125.8 jit_solution(17295871042197257378)
XLA Ops:
  0.6 2.3 %shard_map.68 = (bf16[2400,128]{1,0:T(8,128)(2,1)S(1)}, bf16[3936,128]{1,0:T(8,128)(2,1)S(1)}, bf16[2016,128]{1,0:T(8,128)(2,1)S(1)}, bf16[384,128]{1,0:T(8,128)...) custom-call(s32[1]{0:T(128)} %bitcast.place_ref, ...), custom_call_target="tpu_custom_call" | custom-call | bytes 7376896 | tf_op jit(solution)/shard_map/pallas_call | solution.py:103
  2.9 3.1 %collective-permute-start = (bf16[3936,128]{1,0:T(8,128)(2,1)S(1)}, bf16[3936,128]{1,0:T(8,128)(2,1)S(1)}, u32[]{:S(2)}, u32[]{:S(2)}) collective-permute-start(bf16[3936,128]{1,0:T(8,128)(2,1)S(1)} %get-tuple-element.31), channel_id=1, source_target_pairs={{0,1},{1,0},{2,3},{3,2},{4,5},{5,4},{6,7},{7,6},{8,9},{9,8},{10,11... | collective-permute-start | bytes 3022856 | tf_op jit(solution)/shard_map/ppermute | solution.py:373
  6.1 2.5 %collective-permute-start.1 = (bf16[2016,128]{1,0:T(8,128)(2,1)S(1)}, bf16[2016,128]{1,0:T(8,128)(2,1)S(1)}, u32[]{:S(2)}, u32[]{:S(2)}) collective-permute-start(bf16[2016,128]{1,0:T(8,128)(2,1)S(1)} %get-tuple-element.33), channel_id=1, source_target_pairs={{0,3},{1,2},{2,1},{3,0},{4,7},{5,6},{6,5},{7,4},{8,11},{9,10},{10,... | collective-permute-start | bytes 1548296 | tf_op jit(solution)/shard_map/ppermute | solution.py:373
  8.5 0.1 collective-permute-start.2
  8.7 2.9 %collective-permute-start.3 = (bf16[384,128]{1,0:T(8,128)(2,1)S(1)}, bf16[384,128]{1,0:T(8,128)(2,1)S(1)}, u32[]{:S(2)}, u32[]{:S(2)}) collective-permute-start(bf16[384,128]{1,0:T(8,128)(2,1)S(1)} %get-tuple-element.40), channel_id=1, source_target_pairs={{0,3},{1,2},{2,1},{3,0},{4,7},{5,6},{6,5},{7,4},{8,11},{9,10},{10,... | collective-permute-start | bytes 294920 | tf_op jit(solution)/shard_map/ppermute | solution.py:373
  11.6 0.3 collective-permute-start.4
  11.9 30.9 %collective-permute-done.1.refs_2_ = bf16[2016,128]{1,0:T(8,128)(2,1)S(1)} collective-permute-done((bf16[2016,128]{1,0:T(8,128)(2,1)S(1)}, bf16[2016,128]{1,0:T(8,128)(2,1)S(1)}, u32[]{:S(2)}, u32[]{:S(2)}) %collective-permute-start.1) | collective-permute-done | bytes 516128 | tf_op jit(solution)/shard_map/ppermute | solution.py:373
  42.8 15.9 %collective-permute-done.2.refs_3_ = bf16[2016,128]{1,0:T(8,128)(2,1)S(1)} collective-permute-done((bf16[2016,128]{1,0:T(8,128)(2,1)S(1)}, bf16[2016,128]{1,0:T(8,128)(2,1)S(1)}, u32[]{:S(2)}, u32[]{:S(2)}) %collective-permute-start.2) | collective-permute-done | bytes 516128 | tf_op jit(solution)/shard_map/ppermute | solution.py:373
  58.7 1.2 shard_map.69
  59.9 1.9 %collective-permute-done.4.refs_8_ = bf16[384,128]{1,0:T(8,128)(2,1)S(1)} collective-permute-done((bf16[384,128]{1,0:T(8,128)(2,1)S(1)}, bf16[384,128]{1,0:T(8,128)(2,1)S(1)}, u32[]{:S(2)}, u32[]{:S(2)}) %collective-permute-start.4) | collective-permute-done | bytes 98336 | tf_op jit(solution)/shard_map/ppermute | solution.py:373
  61.8 2.3 %shard_map.70 = (bf16[384,512]{1,0:T(8,128)(2,1)S(1)}, bf16[384,384]{1,0:T(8,128)(2,1)S(1)}, bf16[192,896]{1,0:T(8,128)(2,1)S(1)}, bf16[192,512]{1,0:T(8,128)(2,...) custom-call(s32[1]{0:T(128)} %bitcast.place_ref, ...), custom_call_target="tpu_custom_call" | custom-call | flops 1207959552 | bytes 5963776 | tf_op jit(solution)/shard_map/pallas_call | solution.py:103
  64.1 0.8 collective-permute-start.7
  64.8 2.2 %collective-permute-start.6 = (bf16[384,256]{1,0:T(8,128)(2,1)S(1)}, bf16[384,256]{1,0:T(8,128)(2,1)S(1)}, u32[]{:S(2)}, u32[]{:S(2)}) collective-permute-start(bf16[384,256]{1,0:T(8,128)(2,1)S(1)} %get-tuple-element.35.refs_4_.first), channel_id=1, source_target_pairs={{0,2},{1,3},{2,0},{3,1},{4,6},{5,7},{6,4},{7,5},{8,10},{9,11},{10,... | collective-permute-start | bytes 589832 | tf_op jit(solution)/shard_map/ppermute | solution.py:373
  67.1 0.7 collective-permute-start.8
  67.8 1.1 shard_map.71
  68.9 2.6 %collective-permute-start.5 = (bf16[256,384]{1,0:T(8,128)(2,1)S(1)}, bf16[256,384]{1,0:T(8,128)(2,1)S(1)}, u32[]{:S(2)}, u32[]{:S(2)}) collective-permute-start(bf16[256,384]{1,0:T(8,128)(2,1)S(1)} %get-tuple-element.45), channel_id=1, source_target_pairs={{0,1},{1,0},{2,3},{3,2},{4,5},{5,4},{6,7},{7,6},{8,9},{9,8},{10,11... | collective-permute-start | bytes 589832 | tf_op jit(solution)/shard_map/ppermute | solution.py:373
  71.5 0.1 collective-permute-start.9
  71.6 24.1 %collective-permute-done.6.first = bf16[384,256]{1,0:T(8,128)(2,1)S(1)} collective-permute-done((bf16[384,256]{1,0:T(8,128)(2,1)S(1)}, bf16[384,256]{1,0:T(8,128)(2,1)S(1)}, u32[]{:S(2)}, u32[]{:S(2)}) %collective-permute-start.6) | collective-permute-done | bytes 196640 | tf_op jit(solution)/shard_map/ppermute | solution.py:373
  95.6 0.0 collective-permute-start.10
  95.6 0.0 collective-permute-done.7.near
  95.7 8.3 %collective-permute-done.10.far = bf16[192,128]{1,0:T(8,128)(2,1)S(1)} collective-permute-done((bf16[192,128]{1,0:T(8,128)(2,1)S(1)}, bf16[192,128]{1,0:T(8,128)(2,1)S(1)}, u32[]{:S(2)}, u32[]{:S(2)}) %collective-permute-start.10) | collective-permute-done | bytes 49184 | tf_op jit(solution)/shard_map/ppermute | solution.py:373
  104.0 0.0 collective-permute-start.15
  104.0 2.8 %collective-permute-start.16 = (bf16[3,96,384]{2,1,0:T(8,128)(2,1)S(1)}, bf16[3,96,384]{2,1,0:T(8,128)(2,1)S(1)}, u32[]{:S(2)}, u32[]{:S(2)}) collective-permute-start(bf16[3,96,384]{2,1,0:T(8,128)(2,1)S(1)} %get-tuple-element.57), channel_id=1, source_target_pairs={{0,5},{1,4},{2,7},{3,6},{4,9},{5,8},{6,11},{7,10},{8,13},{9,12},{1... | collective-permute-start | bytes 663560 | tf_op jit(solution)/shard_map/ppermute | solution.py:381
  106.8 0.6 shard_map.72.hidden
  107.4 0.3 shard_map.74
  107.7 0.4 collective-permute-start.12
  108.2 0.3 shard_map.73
  108.5 8.8 %collective-permute-done.12.mate1 = bf16[256,128]{1,0:T(8,128)(2,1)S(1)} collective-permute-done((bf16[256,128]{1,0:T(8,128)(2,1)S(1)}, bf16[256,128]{1,0:T(8,128)(2,1)S(1)}, u32[]{:S(2)}, u32[]{:S(2)}) %collective-permute-start.12) | collective-permute-done | bytes 65568 | tf_op jit(solution)/shard_map/ppermute | solution.py:373
  117.3 0.4 collective-permute-start.11
  117.7 5.7 %collective-permute-done.11.mate0 = bf16[256,256]{1,0:T(8,128)(2,1)S(1)} collective-permute-done((bf16[256,256]{1,0:T(8,128)(2,1)S(1)}, bf16[256,256]{1,0:T(8,128)(2,1)S(1)}, u32[]{:S(2)}, u32[]{:S(2)}) %collective-permute-start.11) | collective-permute-done | bytes 131104 | tf_op jit(solution)/shard_map/ppermute | solution.py:373
  123.5 1.0 shard_map.75
  124.4 1.3 %shard_map.77 = f32[1,4,3,96,384]{4,3,2,1,0:T(8,128)} custom-call(s32[1]{0:T(128)} %bitcast.place_ref, bf16[3,96,384]{2,1,0:T(8,128)(2,1)S(1)} %collective-permute-done.13.refs_0_, bf16[3,96,384]{2,1,0:T(8,128)(2,1)S(1)} %collective-permute-done.14.refs_1_, bf16[3,96,384]{2,1,0:T(8,128)(2,1)S(1)} %collective-permute-done.15.refs_2_, ...), custom_call_target="tpu_custom_call" | custom-call | bytes 2654208 | tf_op jit(solution)/shard_map/pallas_call | solution.py:103
  (12 shorter events, 0.1 us)
Async XLA Ops:
  2.9 55.7 %collective-permute-start = (bf16[3936,128]{1,0:T(8,128)(2,1)S(1)}, bf16[3936,128]{1,0:T(8,128)(2,1)S(1)}, u32[]{:S(2)}, u32[]{:S(2)}) collective-permute-start(bf16[3936,128]{1,0:T(8,128)(2,1)S(1)} %get-tuple-element.31), channel_id=1, source_target_pairs={{0,1},{1,0},{2,3},{3,2},{4,5},{5,4},{6,7},{7,6},{8,9},{9,8},{10,11... | collective-permute-start | bytes 3022856 | tf_op jit(solution)/shard_map/ppermute | solution.py:373
  6.1 36.8 %collective-permute-start.1 = (bf16[2016,128]{1,0:T(8,128)(2,1)S(1)}, bf16[2016,128]{1,0:T(8,128)(2,1)S(1)}, u32[]{:S(2)}, u32[]{:S(2)}) collective-permute-start(bf16[2016,128]{1,0:T(8,128)(2,1)S(1)} %get-tuple-element.33), channel_id=1, source_target_pairs={{0,3},{1,2},{2,1},{3,0},{4,7},{5,6},{6,5},{7,4},{8,11},{9,10},{10,... | collective-permute-start | bytes 1548296 | tf_op jit(solution)/shard_map/ppermute | solution.py:373
  8.5 50.1 %collective-permute-start.2 = (bf16[2016,128]{1,0:T(8,128)(2,1)S(1)}, bf16[2016,128]{1,0:T(8,128)(2,1)S(1)}, u32[]{:S(2)}, u32[]{:S(2)}) collective-permute-start(bf16[2016,128]{1,0:T(8,128)(2,1)S(1)} %get-tuple-element.34), channel_id=1, source_target_pairs={{0,2},{1,3},{2,0},{3,1},{4,6},{5,7},{6,4},{7,5},{8,10},{9,11},{10,... | collective-permute-start | bytes 1548296 | tf_op jit(solution)/shard_map/ppermute | solution.py:373
  8.7 51.2 %collective-permute-start.3 = (bf16[384,128]{1,0:T(8,128)(2,1)S(1)}, bf16[384,128]{1,0:T(8,128)(2,1)S(1)}, u32[]{:S(2)}, u32[]{:S(2)}) collective-permute-start(bf16[384,128]{1,0:T(8,128)(2,1)S(1)} %get-tuple-element.40), channel_id=1, source_target_pairs={{0,3},{1,2},{2,1},{3,0},{4,7},{5,6},{6,5},{7,4},{8,11},{9,10},{10,... | collective-permute-start | bytes 294920 | tf_op jit(solution)/shard_map/ppermute | solution.py:373
  11.6 50.2 %collective-permute-start.4 = (bf16[384,128]{1,0:T(8,128)(2,1)S(1)}, bf16[384,128]{1,0:T(8,128)(2,1)S(1)}, u32[]{:S(2)}, u32[]{:S(2)}) collective-permute-start(bf16[384,128]{1,0:T(8,128)(2,1)S(1)} %get-tuple-element.41), channel_id=1, source_target_pairs={{0,2},{1,3},{2,0},{3,1},{4,6},{5,7},{6,4},{7,5},{8,10},{9,11},{10,... | collective-permute-start | bytes 294920 | tf_op jit(solution)/shard_map/ppermute | solution.py:373
  64.1 31.6 %collective-permute-start.7 = (bf16[192,896]{1,0:T(8,128)(2,1)S(1)}, bf16[192,896]{1,0:T(8,128)(2,1)S(1)}, u32[]{:S(2)}, u32[]{:S(2)}) collective-permute-start(bf16[192,896]{1,0:T(8,128)(2,1)S(1)} %get-tuple-element.46), channel_id=1, source_target_pairs={{0,2},{1,3},{2,0},{3,1},{4,6},{5,7},{6,4},{7,5},{8,10},{9,11},{10,... | collective-permute-start | bytes 1032200 | tf_op jit(solution)/shard_map/ppermute | solution.py:373
  64.8 30.8 %collective-permute-start.6 = (bf16[384,256]{1,0:T(8,128)(2,1)S(1)}, bf16[384,256]{1,0:T(8,128)(2,1)S(1)}, u32[]{:S(2)}, u32[]{:S(2)}) collective-permute-start(bf16[384,256]{1,0:T(8,128)(2,1)S(1)} %get-tuple-element.35.refs_4_.first), channel_id=1, source_target_pairs={{0,2},{1,3},{2,0},{3,1},{4,6},{5,7},{6,4},{7,5},{8,10},{9,11},{10,... | collective-permute-start | bytes 589832 | tf_op jit(solution)/shard_map/ppermute | solution.py:373
  67.1 36.9 %collective-permute-start.8 = (bf16[192,512]{1,0:T(8,128)(2,1)S(1)}, bf16[192,512]{1,0:T(8,128)(2,1)S(1)}, u32[]{:S(2)}, u32[]{:S(2)}) collective-permute-start(bf16[192,512]{1,0:T(8,128)(2,1)S(1)} %get-tuple-element.47), channel_id=1, source_target_pairs={{0,2},{1,3},{2,0},{3,1},{4,6},{5,7},{6,4},{7,5},{8,10},{9,11},{10,... | collective-permute-start | bytes 589832 | tf_op jit(solution)/shard_map/ppermute | solution.py:373
  68.9 38.8 %collective-permute-start.5 = (bf16[256,384]{1,0:T(8,128)(2,1)S(1)}, bf16[256,384]{1,0:T(8,128)(2,1)S(1)}, u32[]{:S(2)}, u32[]{:S(2)}) collective-permute-start(bf16[256,384]{1,0:T(8,128)(2,1)S(1)} %get-tuple-element.45), channel_id=1, source_target_pairs={{0,1},{1,0},{2,3},{3,2},{4,5},{5,4},{6,7},{7,6},{8,9},{9,8},{10,11... | collective-permute-start | bytes 589832 | tf_op jit(solution)/shard_map/ppermute | solution.py:373
  71.5 32.5 %collective-permute-start.9 = (bf16[192,256]{1,0:T(8,128)(2,1)S(1)}, bf16[192,256]{1,0:T(8,128)(2,1)S(1)}, u32[]{:S(2)}, u32[]{:S(2)}) collective-permute-start(bf16[192,256]{1,0:T(8,128)(2,1)S(1)} %get-tuple-element.48), channel_id=1, source_target_pairs={{0,2},{1,3},{2,0},{3,1},{4,6},{5,7},{6,4},{7,5},{8,10},{9,11},{10,... | collective-permute-start | bytes 294920 | tf_op jit(solution)/shard_map/ppermute | solution.py:373
  95.6 8.3 %collective-permute-start.10 = (bf16[192,128]{1,0:T(8,128)(2,1)S(1)}, bf16[192,128]{1,0:T(8,128)(2,1)S(1)}, u32[]{:S(2)}, u32[]{:S(2)}) collective-permute-start(bf16[192,128]{1,0:T(8,128)(2,1)S(1)} %get-tuple-element.50), channel_id=1, source_target_pairs={{0,2},{1,3},{2,0},{3,1},{4,6},{5,7},{6,4},{7,5},{8,10},{9,11},{10,... | collective-permute-start | bytes 147464 | tf_op jit(solution)/shard_map/ppermute | solution.py:373
  95.6 28.8 %collective-permute-start.13 = (bf16[3,96,384]{2,1,0:T(8,128)(2,1)S(1)}, bf16[3,96,384]{2,1,0:T(8,128)(2,1)S(1)}, u32[]{:S(2)}, u32[]{:S(2)}) collective-permute-start(bf16[3,96,384]{2,1,0:T(8,128)(2,1)S(1)} %get-tuple-element.54), channel_id=1, source_target_pairs={{0,4},{1,5},{2,6},{3,7},{4,8},{5,9},{6,10},{7,11},{8,12},{9,13},{1... | collective-permute-start | bytes 663560 | tf_op jit(solution)/shard_map/ppermute | solution.py:381
  104.0 20.5 %collective-permute-start.14 = (bf16[3,96,384]{2,1,0:T(8,128)(2,1)S(1)}, bf16[3,96,384]{2,1,0:T(8,128)(2,1)S(1)}, u32[]{:S(2)}, u32[]{:S(2)}) collective-permute-start(bf16[3,96,384]{2,1,0:T(8,128)(2,1)S(1)} %get-tuple-element.55), channel_id=1, source_target_pairs={{0,5},{1,4},{2,7},{3,6},{4,9},{5,8},{6,11},{7,10},{8,13},{9,12},{1... | collective-permute-start | bytes 663560 | tf_op jit(solution)/shard_map/ppermute | solution.py:381
  104.0 20.4 %collective-permute-start.15 = (bf16[3,96,384]{2,1,0:T(8,128)(2,1)S(1)}, bf16[3,96,384]{2,1,0:T(8,128)(2,1)S(1)}, u32[]{:S(2)}, u32[]{:S(2)}) collective-permute-start(bf16[3,96,384]{2,1,0:T(8,128)(2,1)S(1)} %get-tuple-element.56), channel_id=1, source_target_pairs={{0,4},{1,5},{2,6},{3,7},{4,8},{5,9},{6,10},{7,11},{8,12},{9,13},{1... | collective-permute-start | bytes 663560 | tf_op jit(solution)/shard_map/ppermute | solution.py:381
  104.0 20.4 %collective-permute-start.16 = (bf16[3,96,384]{2,1,0:T(8,128)(2,1)S(1)}, bf16[3,96,384]{2,1,0:T(8,128)(2,1)S(1)}, u32[]{:S(2)}, u32[]{:S(2)}) collective-permute-start(bf16[3,96,384]{2,1,0:T(8,128)(2,1)S(1)} %get-tuple-element.57), channel_id=1, source_target_pairs={{0,5},{1,4},{2,7},{3,6},{4,9},{5,8},{6,11},{7,10},{8,13},{9,12},{1... | collective-permute-start | bytes 663560 | tf_op jit(solution)/shard_map/ppermute | solution.py:381
  107.7 9.6 %collective-permute-start.12 = (bf16[256,128]{1,0:T(8,128)(2,1)S(1)}, bf16[256,128]{1,0:T(8,128)(2,1)S(1)}, u32[]{:S(2)}, u32[]{:S(2)}) collective-permute-start(bf16[256,128]{1,0:T(8,128)(2,1)S(1)} %get-tuple-element.53), channel_id=1, source_target_pairs={{0,1},{1,0},{2,3},{3,2},{4,5},{5,4},{6,7},{7,6},{8,9},{9,8},{10,11... | collective-permute-start | bytes 196616 | tf_op jit(solution)/shard_map/ppermute | solution.py:373
  117.3 6.2 %collective-permute-start.11 = (bf16[256,256]{1,0:T(8,128)(2,1)S(1)}, bf16[256,256]{1,0:T(8,128)(2,1)S(1)}, u32[]{:S(2)}, u32[]{:S(2)}) collective-permute-start(bf16[256,256]{1,0:T(8,128)(2,1)S(1)} %get-tuple-element.52), channel_id=1, source_target_pairs={{0,1},{1,0},{2,3},{3,2},{4,5},{5,4},{6,7},{7,6},{8,9},{9,8},{10,11... | collective-permute-start | bytes 393224 | tf_op jit(solution)/shard_map/ppermute | solution.py:373

commit v3 on v2

--- a/solution.py
+++ b/solution.py
@@ -184,12 +184,12 @@
                 head, 2, :, c * LANES : (c + 1) * LANES
             ].astype(jnp.bfloat16)
     copies[4].wait()
-    for i, head in enumerate((here ^ 1, here ^ 3)):
+    for i, head in enumerate((here ^ 1, here ^ 2)):
         for c in range(blocks):
             at = span(head * width + c * LANES, LANES, LANES)
             start = sizes.query_at + (i * blocks + c) * tokens
             mate_ref[start : start + tokens] = queries_ref[:, at]
-    for i, head in enumerate((here, here ^ 2)):
+    for i, head in enumerate((here, here ^ 3)):
         query_ref[i] = queries_ref[:, span(head * width, width, LANES)]
 
 
@@ -344,7 +344,7 @@
 
 def handed_kernel(place_ref, *refs):
     here = place_ref[0]
-    for head, ref in zip((here, here ^ 1, here ^ 2, here ^ 3), refs[:4]):
+    for head, ref in zip((here, here ^ 1, here ^ 3, here ^ 2), refs[:4]):
         refs[4][0, head] = ref[...].astype(jnp.float32)
 
 
@@ -352,7 +352,7 @@
     here, width, late = place_ref[0], sizes.width, sizes.late_width
     applied_ref[:, span(here * width, width, LANES)] = own[...]
     applied_ref[:, span((here ^ 1) * width, width, LANES)] = mate[...]
-    for head, (first, second) in ((here ^ 2, (own0, own1)), (here ^ 3, (mate0, mate1))):
+    for head, (first, second) in ((here ^ 3, (own0, own1)), (here ^ 2, (mate0, mate1))):
         applied_ref[:, span(head * width, late, LANES)] = first[...]
         applied_ref[:, span(head * width + late, LANES, LANES)] = second[...]
 
@@ -421,7 +421,7 @@
         (own, mate, cross, other),
         6 * heads * flops // 3,
     )
-    first_in = swapped(first, 2)
+    first_in = swapped(first, 3)
     second, down, near, far, far0, far1, same_rows, mate_rows = call(
         functools.partial(second_kernel, sizes),
         [
@@ -443,10 +443,10 @@
         (keys, targets, down, early, first, own, mate, cross_late, other_late),
         12 * heads * flops // 3,
     )
-    near_in = swapped(near, 2)
-    far_in = swapped(far, 2)
-    far0_in = swapped(far0, 2)
-    far1_in = swapped(far1, 2)
+    near_in = swapped(near, 3)
+    far_in = swapped(far, 3)
+    far0_in = swapped(far0, 3)
+    far1_in = swapped(far1, 3)
     own_result, mate_result = call(
         functools.partial(own_kernel, sizes),
         [bf16(tokens, width)] * 2,

time: 126 us -> 122 us (0.968)
  waiting for transfers between devices: 95.6 us -> 74.3 us
  starting transfers between devices: 19.1 us -> 36.1 us
    ppermute x13, waiting for transfers between devices: 95.5 us -> 74.3 us  [swapped(): return lax.ppermute(value, 'tok', [(i, i ^ mask) for i in range(heads)])]
    ppermute x4, starting transfers between devices: 2.86 us -> 13.8 us  [next_block(): return lax.ppermute(value, ('block', 'tok'), route)]
    ppermute x13, starting transfers between devices: 16.2 us -> 22.2 us  [swapped(): return lax.ppermute(value, 'tok', [(i, i ^ mask) for i in range(heads)])]
where the time goes in v3:
time: 122 us; the launch traced here: 121 us
  waiting for transfers between devices  74.3 us (61%)
  starting transfers between devices  36.1 us (30%)
  Pallas kernels  10.4 us (9%)
    ppermute x13, waiting for transfers between devices, swapped(): return lax.ppermute(value, 'tok', [(i, i ^ mask) for i in range(heads)])  74.3 us
    ppermute x13, starting transfers between devices, swapped(): return lax.ppermute(value, 'tok', [(i, i ^ mask) for i in range(heads)])  22.2 us
    ppermute x4, starting transfers between devices, next_block(): return lax.ppermute(value, ('block', 'tok'), route)  13.8 us
    pallas_call x10, Pallas kernels, call(): return run(place, *args)  10.4 us
  transfers between devices with their start and end apart: 17, of which 7 were waited for; matrix products, arithmetic and copies ran while one was open for 0% of the time, Pallas kernels for 4%

profile of v3, /device:TPU:0, one launch (start us, length us, event | category | flops | bytes accessed | tf_op | source)
XLA Modules:
  0.0 121.5 jit_solution(5541500662405707137)
XLA Ops:
  0.6 2.3 %shard_map.68 = (bf16[2400,128]{1,0:T(8,128)(2,1)S(1)}, bf16[3936,128]{1,0:T(8,128)(2,1)S(1)}, bf16[2016,128]{1,0:T(8,128)(2,1)S(1)}, bf16[384,128]{1,0:T(8,128)...) custom-call(s32[1]{0:T(128)} %bitcast.place_ref, ...), custom_call_target="tpu_custom_call" | custom-call | bytes 7376896 | tf_op jit(solution)/shard_map/pallas_call | solution.py:103
  2.9 3.1 %collective-permute-start = (bf16[3936,128]{1,0:T(8,128)(2,1)S(1)}, bf16[3936,128]{1,0:T(8,128)(2,1)S(1)}, u32[]{:S(2)}, u32[]{:S(2)}) collective-permute-start(bf16[3936,128]{1,0:T(8,128)(2,1)S(1)} %get-tuple-element.31), channel_id=1, source_target_pairs={{0,1},{1,0},{2,3},{3,2},{4,5},{5,4},{6,7},{7,6},{8,9},{9,8},{10,11... | collective-permute-start | bytes 3022856 | tf_op jit(solution)/shard_map/ppermute | solution.py:373
  6.1 2.5 %collective-permute-start.1 = (bf16[2016,128]{1,0:T(8,128)(2,1)S(1)}, bf16[2016,128]{1,0:T(8,128)(2,1)S(1)}, u32[]{:S(2)}, u32[]{:S(2)}) collective-permute-start(bf16[2016,128]{1,0:T(8,128)(2,1)S(1)} %get-tuple-element.33), channel_id=1, source_target_pairs={{0,3},{1,2},{2,1},{3,0},{4,7},{5,6},{6,5},{7,4},{8,11},{9,10},{10,... | collective-permute-start | bytes 1548296 | tf_op jit(solution)/shard_map/ppermute | solution.py:373
  8.5 0.1 collective-permute-start.2
  8.7 2.9 %collective-permute-start.3 = (bf16[384,128]{1,0:T(8,128)(2,1)S(1)}, bf16[384,128]{1,0:T(8,128)(2,1)S(1)}, u32[]{:S(2)}, u32[]{:S(2)}) collective-permute-start(bf16[384,128]{1,0:T(8,128)(2,1)S(1)} %get-tuple-element.40), channel_id=1, source_target_pairs={{0,3},{1,2},{2,1},{3,0},{4,7},{5,6},{6,5},{7,4},{8,11},{9,10},{10,... | collective-permute-start | bytes 294920 | tf_op jit(solution)/shard_map/ppermute | solution.py:373
  11.6 0.3 collective-permute-start.4
  11.9 30.9 %collective-permute-done.1.refs_2_ = bf16[2016,128]{1,0:T(8,128)(2,1)S(1)} collective-permute-done((bf16[2016,128]{1,0:T(8,128)(2,1)S(1)}, bf16[2016,128]{1,0:T(8,128)(2,1)S(1)}, u32[]{:S(2)}, u32[]{:S(2)}) %collective-permute-start.1) | collective-permute-done | bytes 516128 | tf_op jit(solution)/shard_map/ppermute | solution.py:373
  42.8 15.9 %collective-permute-done.2.refs_3_ = bf16[2016,128]{1,0:T(8,128)(2,1)S(1)} collective-permute-done((bf16[2016,128]{1,0:T(8,128)(2,1)S(1)}, bf16[2016,128]{1,0:T(8,128)(2,1)S(1)}, u32[]{:S(2)}, u32[]{:S(2)}) %collective-permute-start.2) | collective-permute-done | bytes 516128 | tf_op jit(solution)/shard_map/ppermute | solution.py:373
  58.7 1.2 shard_map.69
  59.9 1.9 %collective-permute-done.4.refs_8_ = bf16[384,128]{1,0:T(8,128)(2,1)S(1)} collective-permute-done((bf16[384,128]{1,0:T(8,128)(2,1)S(1)}, bf16[384,128]{1,0:T(8,128)(2,1)S(1)}, u32[]{:S(2)}, u32[]{:S(2)}) %collective-permute-start.4) | collective-permute-done | bytes 98336 | tf_op jit(solution)/shard_map/ppermute | solution.py:373
  61.8 2.3 %shard_map.70 = (bf16[384,512]{1,0:T(8,128)(2,1)S(1)}, bf16[384,384]{1,0:T(8,128)(2,1)S(1)}, bf16[192,896]{1,0:T(8,128)(2,1)S(1)}, bf16[192,512]{1,0:T(8,128)(2,...) custom-call(s32[1]{0:T(128)} %bitcast.place_ref, ...), custom_call_target="tpu_custom_call" | custom-call | flops 1207959552 | bytes 5963776 | tf_op jit(solution)/shard_map/pallas_call | solution.py:103
  64.1 2.7 %collective-permute-start.7 = (bf16[192,896]{1,0:T(8,128)(2,1)S(1)}, bf16[192,896]{1,0:T(8,128)(2,1)S(1)}, u32[]{:S(2)}, u32[]{:S(2)}) collective-permute-start(bf16[192,896]{1,0:T(8,128)(2,1)S(1)} %get-tuple-element.46), channel_id=1, source_target_pairs={{0,3},{1,2},{2,1},{3,0},{4,7},{5,6},{6,5},{7,4},{8,11},{9,10},{10,... | collective-permute-start | bytes 1032200 | tf_op jit(solution)/shard_map/ppermute | solution.py:373
  66.8 1.2 collective-permute-start.6
  68.0 2.6 %collective-permute-start.8 = (bf16[192,512]{1,0:T(8,128)(2,1)S(1)}, bf16[192,512]{1,0:T(8,128)(2,1)S(1)}, u32[]{:S(2)}, u32[]{:S(2)}) collective-permute-start(bf16[192,512]{1,0:T(8,128)(2,1)S(1)} %get-tuple-element.47), channel_id=1, source_target_pairs={{0,3},{1,2},{2,1},{3,0},{4,7},{5,6},{6,5},{7,4},{8,11},{9,10},{10,... | collective-permute-start | bytes 589832 | tf_op jit(solution)/shard_map/ppermute | solution.py:373
  70.6 1.1 shard_map.71
  71.7 0.1 collective-permute-start.5
  71.8 1.2 %collective-permute-start.9 = (bf16[192,256]{1,0:T(8,128)(2,1)S(1)}, bf16[192,256]{1,0:T(8,128)(2,1)S(1)}, u32[]{:S(2)}, u32[]{:S(2)}) collective-permute-start(bf16[192,256]{1,0:T(8,128)(2,1)S(1)} %get-tuple-element.48), channel_id=1, source_target_pairs={{0,3},{1,2},{2,1},{3,0},{4,7},{5,6},{6,5},{7,4},{8,11},{9,10},{10,... | collective-permute-start | bytes 294920 | tf_op jit(solution)/shard_map/ppermute | solution.py:373
  73.1 8.1 %collective-permute-done.6.first = bf16[384,256]{1,0:T(8,128)(2,1)S(1)} collective-permute-done((bf16[384,256]{1,0:T(8,128)(2,1)S(1)}, bf16[384,256]{1,0:T(8,128)(2,1)S(1)}, u32[]{:S(2)}, u32[]{:S(2)}) %collective-permute-start.6) | collective-permute-done | bytes 196640 | tf_op jit(solution)/shard_map/ppermute | solution.py:373
  81.1 2.6 %collective-permute-start.10 = (bf16[192,128]{1,0:T(8,128)(2,1)S(1)}, bf16[192,128]{1,0:T(8,128)(2,1)S(1)}, u32[]{:S(2)}, u32[]{:S(2)}) collective-permute-start(bf16[192,128]{1,0:T(8,128)(2,1)S(1)} %get-tuple-element.50), channel_id=1, source_target_pairs={{0,3},{1,2},{2,1},{3,0},{4,7},{5,6},{6,5},{7,4},{8,11},{9,10},{10,... | collective-permute-start | bytes 147464 | tf_op jit(solution)/shard_map/ppermute | solution.py:373
  83.8 6.8 %collective-permute-done.10.far = bf16[192,128]{1,0:T(8,128)(2,1)S(1)} collective-permute-done((bf16[192,128]{1,0:T(8,128)(2,1)S(1)}, bf16[192,128]{1,0:T(8,128)(2,1)S(1)}, u32[]{:S(2)}, u32[]{:S(2)}) %collective-permute-start.10) | collective-permute-done | bytes 49184 | tf_op jit(solution)/shard_map/ppermute | solution.py:373
  90.6 10.2 %collective-permute-start.14 = (bf16[3,96,384]{2,1,0:T(8,128)(2,1)S(1)}, bf16[3,96,384]{2,1,0:T(8,128)(2,1)S(1)}, u32[]{:S(2)}, u32[]{:S(2)}) collective-permute-start(bf16[3,96,384]{2,1,0:T(8,128)(2,1)S(1)} %get-tuple-element.55), channel_id=1, source_target_pairs={{0,5},{1,4},{2,7},{3,6},{4,9},{5,8},{6,11},{7,10},{8,13},{9,12},{1... | collective-permute-start | bytes 663560 | tf_op jit(solution)/shard_map/ppermute | solution.py:381
  100.8 3.4 %collective-permute-start.15 = (bf16[3,96,384]{2,1,0:T(8,128)(2,1)S(1)}, bf16[3,96,384]{2,1,0:T(8,128)(2,1)S(1)}, u32[]{:S(2)}, u32[]{:S(2)}) collective-permute-start(bf16[3,96,384]{2,1,0:T(8,128)(2,1)S(1)} %get-tuple-element.56), channel_id=1, source_target_pairs={{0,4},{1,5},{2,6},{3,7},{4,8},{5,9},{6,10},{7,11},{8,12},{9,13},{1... | collective-permute-start | bytes 663560 | tf_op jit(solution)/shard_map/ppermute | solution.py:381
  104.2 0.2 collective-permute-start.16
  104.4 0.6 shard_map.72.hidden
  105.0 0.3 shard_map.74
  105.3 1.6 %collective-permute-start.12 = (bf16[256,128]{1,0:T(8,128)(2,1)S(1)}, bf16[256,128]{1,0:T(8,128)(2,1)S(1)}, u32[]{:S(2)}, u32[]{:S(2)}) collective-permute-start(bf16[256,128]{1,0:T(8,128)(2,1)S(1)} %get-tuple-element.53), channel_id=1, source_target_pairs={{0,1},{1,0},{2,3},{3,2},{4,5},{5,4},{6,7},{7,6},{8,9},{9,8},{10,11... | collective-permute-start | bytes 196616 | tf_op jit(solution)/shard_map/ppermute | solution.py:373
  106.9 0.3 shard_map.73
  107.2 5.7 %collective-permute-done.12.mate1 = bf16[256,128]{1,0:T(8,128)(2,1)S(1)} collective-permute-done((bf16[256,128]{1,0:T(8,128)(2,1)S(1)}, bf16[256,128]{1,0:T(8,128)(2,1)S(1)}, u32[]{:S(2)}, u32[]{:S(2)}) %collective-permute-start.12) | collective-permute-done | bytes 65568 | tf_op jit(solution)/shard_map/ppermute | solution.py:373
  112.9 1.2 collective-permute-start.11
  114.1 5.1 %collective-permute-done.11.mate0 = bf16[256,256]{1,0:T(8,128)(2,1)S(1)} collective-permute-done((bf16[256,256]{1,0:T(8,128)(2,1)S(1)}, bf16[256,256]{1,0:T(8,128)(2,1)S(1)}, u32[]{:S(2)}, u32[]{:S(2)}) %collective-permute-start.11) | collective-permute-done | bytes 131104 | tf_op jit(solution)/shard_map/ppermute | solution.py:373
  119.2 1.0 shard_map.75
  120.1 1.3 %shard_map.77 = f32[1,4,3,96,384]{4,3,2,1,0:T(8,128)} custom-call(s32[1]{0:T(128)} %bitcast.place_ref, bf16[3,96,384]{2,1,0:T(8,128)(2,1)S(1)} %collective-permute-done.13.refs_0_, bf16[3,96,384]{2,1,0:T(8,128)(2,1)S(1)} %collective-permute-done.14.refs_1_, bf16[3,96,384]{2,1,0:T(8,128)(2,1)S(1)} %collective-permute-done.15.refs_2_, ...), custom_call_target="tpu_custom_call" | custom-call | bytes 2654208 | tf_op jit(solution)/shard_map/pallas_call | solution.py:103
  (12 shorter events, 0.1 us)
Async XLA Ops:
  2.9 55.7 %collective-permute-start = (bf16[3936,128]{1,0:T(8,128)(2,1)S(1)}, bf16[3936,128]{1,0:T(8,128)(2,1)S(1)}, u32[]{:S(2)}, u32[]{:S(2)}) collective-permute-start(bf16[3936,128]{1,0:T(8,128)(2,1)S(1)} %get-tuple-element.31), channel_id=1, source_target_pairs={{0,1},{1,0},{2,3},{3,2},{4,5},{5,4},{6,7},{7,6},{8,9},{9,8},{10,11... | collective-permute-start | bytes 3022856 | tf_op jit(solution)/shard_map/ppermute | solution.py:373
  6.1 36.8 %collective-permute-start.1 = (bf16[2016,128]{1,0:T(8,128)(2,1)S(1)}, bf16[2016,128]{1,0:T(8,128)(2,1)S(1)}, u32[]{:S(2)}, u32[]{:S(2)}) collective-permute-start(bf16[2016,128]{1,0:T(8,128)(2,1)S(1)} %get-tuple-element.33), channel_id=1, source_target_pairs={{0,3},{1,2},{2,1},{3,0},{4,7},{5,6},{6,5},{7,4},{8,11},{9,10},{10,... | collective-permute-start | bytes 1548296 | tf_op jit(solution)/shard_map/ppermute | solution.py:373
  8.5 50.1 %collective-permute-start.2 = (bf16[2016,128]{1,0:T(8,128)(2,1)S(1)}, bf16[2016,128]{1,0:T(8,128)(2,1)S(1)}, u32[]{:S(2)}, u32[]{:S(2)}) collective-permute-start(bf16[2016,128]{1,0:T(8,128)(2,1)S(1)} %get-tuple-element.34), channel_id=1, source_target_pairs={{0,2},{1,3},{2,0},{3,1},{4,6},{5,7},{6,4},{7,5},{8,10},{9,11},{10,... | collective-permute-start | bytes 1548296 | tf_op jit(solution)/shard_map/ppermute | solution.py:373
  8.7 51.2 %collective-permute-start.3 = (bf16[384,128]{1,0:T(8,128)(2,1)S(1)}, bf16[384,128]{1,0:T(8,128)(2,1)S(1)}, u32[]{:S(2)}, u32[]{:S(2)}) collective-permute-start(bf16[384,128]{1,0:T(8,128)(2,1)S(1)} %get-tuple-element.40), channel_id=1, source_target_pairs={{0,3},{1,2},{2,1},{3,0},{4,7},{5,6},{6,5},{7,4},{8,11},{9,10},{10,... | collective-permute-start | bytes 294920 | tf_op jit(solution)/shard_map/ppermute | solution.py:373
  11.6 50.2 %collective-permute-start.4 = (bf16[384,128]{1,0:T(8,128)(2,1)S(1)}, bf16[384,128]{1,0:T(8,128)(2,1)S(1)}, u32[]{:S(2)}, u32[]{:S(2)}) collective-permute-start(bf16[384,128]{1,0:T(8,128)(2,1)S(1)} %get-tuple-element.41), channel_id=1, source_target_pairs={{0,2},{1,3},{2,0},{3,1},{4,6},{5,7},{6,4},{7,5},{8,10},{9,11},{10,... | collective-permute-start | bytes 294920 | tf_op jit(solution)/shard_map/ppermute | solution.py:373
  64.1 19.7 %collective-permute-start.7 = (bf16[192,896]{1,0:T(8,128)(2,1)S(1)}, bf16[192,896]{1,0:T(8,128)(2,1)S(1)}, u32[]{:S(2)}, u32[]{:S(2)}) collective-permute-start(bf16[192,896]{1,0:T(8,128)(2,1)S(1)} %get-tuple-element.46), channel_id=1, source_target_pairs={{0,3},{1,2},{2,1},{3,0},{4,7},{5,6},{6,5},{7,4},{8,11},{9,10},{10,... | collective-permute-start | bytes 1032200 | tf_op jit(solution)/shard_map/ppermute | solution.py:373
  66.8 14.3 %collective-permute-start.6 = (bf16[384,256]{1,0:T(8,128)(2,1)S(1)}, bf16[384,256]{1,0:T(8,128)(2,1)S(1)}, u32[]{:S(2)}, u32[]{:S(2)}) collective-permute-start(bf16[384,256]{1,0:T(8,128)(2,1)S(1)} %get-tuple-element.35.refs_4_.first), channel_id=1, source_target_pairs={{0,3},{1,2},{2,1},{3,0},{4,7},{5,6},{6,5},{7,4},{8,11},{9,10},{10,... | collective-permute-start | bytes 589832 | tf_op jit(solution)/shard_map/ppermute | solution.py:373
  68.0 36.3 %collective-permute-start.8 = (bf16[192,512]{1,0:T(8,128)(2,1)S(1)}, bf16[192,512]{1,0:T(8,128)(2,1)S(1)}, u32[]{:S(2)}, u32[]{:S(2)}) collective-permute-start(bf16[192,512]{1,0:T(8,128)(2,1)S(1)} %get-tuple-element.47), channel_id=1, source_target_pairs={{0,3},{1,2},{2,1},{3,0},{4,7},{5,6},{6,5},{7,4},{8,11},{9,10},{10,... | collective-permute-start | bytes 589832 | tf_op jit(solution)/shard_map/ppermute | solution.py:373
  71.7 33.5 %collective-permute-start.5 = (bf16[256,384]{1,0:T(8,128)(2,1)S(1)}, bf16[256,384]{1,0:T(8,128)(2,1)S(1)}, u32[]{:S(2)}, u32[]{:S(2)}) collective-permute-start(bf16[256,384]{1,0:T(8,128)(2,1)S(1)} %get-tuple-element.45), channel_id=1, source_target_pairs={{0,1},{1,0},{2,3},{3,2},{4,5},{5,4},{6,7},{7,6},{8,9},{9,8},{10,11... | collective-permute-start | bytes 589832 | tf_op jit(solution)/shard_map/ppermute | solution.py:373
  71.8 29.0 %collective-permute-start.9 = (bf16[192,256]{1,0:T(8,128)(2,1)S(1)}, bf16[192,256]{1,0:T(8,128)(2,1)S(1)}, u32[]{:S(2)}, u32[]{:S(2)}) collective-permute-start(bf16[192,256]{1,0:T(8,128)(2,1)S(1)} %get-tuple-element.48), channel_id=1, source_target_pairs={{0,3},{1,2},{2,1},{3,0},{4,7},{5,6},{6,5},{7,4},{8,11},{9,10},{10,... | collective-permute-start | bytes 294920 | tf_op jit(solution)/shard_map/ppermute | solution.py:373
  81.1 9.5 %collective-permute-start.10 = (bf16[192,128]{1,0:T(8,128)(2,1)S(1)}, bf16[192,128]{1,0:T(8,128)(2,1)S(1)}, u32[]{:S(2)}, u32[]{:S(2)}) collective-permute-start(bf16[192,128]{1,0:T(8,128)(2,1)S(1)} %get-tuple-element.50), channel_id=1, source_target_pairs={{0,3},{1,2},{2,1},{3,0},{4,7},{5,6},{6,5},{7,4},{8,11},{9,10},{10,... | collective-permute-start | bytes 147464 | tf_op jit(solution)/shard_map/ppermute | solution.py:373
  83.8 36.3 %collective-permute-start.13 = (bf16[3,96,384]{2,1,0:T(8,128)(2,1)S(1)}, bf16[3,96,384]{2,1,0:T(8,128)(2,1)S(1)}, u32[]{:S(2)}, u32[]{:S(2)}) collective-permute-start(bf16[3,96,384]{2,1,0:T(8,128)(2,1)S(1)} %get-tuple-element.54), channel_id=1, source_target_pairs={{0,4},{1,5},{2,6},{3,7},{4,8},{5,9},{6,10},{7,11},{8,12},{9,13},{1... | collective-permute-start | bytes 663560 | tf_op jit(solution)/shard_map/ppermute | solution.py:381
  90.6 29.5 %collective-permute-start.14 = (bf16[3,96,384]{2,1,0:T(8,128)(2,1)S(1)}, bf16[3,96,384]{2,1,0:T(8,128)(2,1)S(1)}, u32[]{:S(2)}, u32[]{:S(2)}) collective-permute-start(bf16[3,96,384]{2,1,0:T(8,128)(2,1)S(1)} %get-tuple-element.55), channel_id=1, source_target_pairs={{0,5},{1,4},{2,7},{3,6},{4,9},{5,8},{6,11},{7,10},{8,13},{9,12},{1... | collective-permute-start | bytes 663560 | tf_op jit(solution)/shard_map/ppermute | solution.py:381
  100.8 19.3 %collective-permute-start.15 = (bf16[3,96,384]{2,1,0:T(8,128)(2,1)S(1)}, bf16[3,96,384]{2,1,0:T(8,128)(2,1)S(1)}, u32[]{:S(2)}, u32[]{:S(2)}) collective-permute-start(bf16[3,96,384]{2,1,0:T(8,128)(2,1)S(1)} %get-tuple-element.56), channel_id=1, source_target_pairs={{0,4},{1,5},{2,6},{3,7},{4,8},{5,9},{6,10},{7,11},{8,12},{9,13},{1... | collective-permute-start | bytes 663560 | tf_op jit(solution)/shard_map/ppermute | solution.py:381
  104.2 15.9 %collective-permute-start.16 = (bf16[3,96,384]{2,1,0:T(8,128)(2,1)S(1)}, bf16[3,96,384]{2,1,0:T(8,128)(2,1)S(1)}, u32[]{:S(2)}, u32[]{:S(2)}) collective-permute-start(bf16[3,96,384]{2,1,0:T(8,128)(2,1)S(1)} %get-tuple-element.57), channel_id=1, source_target_pairs={{0,5},{1,4},{2,7},{3,6},{4,9},{5,8},{6,11},{7,10},{8,13},{9,12},{1... | collective-permute-start | bytes 663560 | tf_op jit(solution)/shard_map/ppermute | solution.py:381
  105.3 7.6 %collective-permute-start.12 = (bf16[256,128]{1,0:T(8,128)(2,1)S(1)}, bf16[256,128]{1,0:T(8,128)(2,1)S(1)}, u32[]{:S(2)}, u32[]{:S(2)}) collective-permute-start(bf16[256,128]{1,0:T(8,128)(2,1)S(1)} %get-tuple-element.53), channel_id=1, source_target_pairs={{0,1},{1,0},{2,3},{3,2},{4,5},{5,4},{6,7},{7,6},{8,9},{9,8},{10,11... | collective-permute-start | bytes 196616 | tf_op jit(solution)/shard_map/ppermute | solution.py:373
  112.9 6.3 %collective-permute-start.11 = (bf16[256,256]{1,0:T(8,128)(2,1)S(1)}, bf16[256,256]{1,0:T(8,128)(2,1)S(1)}, u32[]{:S(2)}, u32[]{:S(2)}) collective-permute-start(bf16[256,256]{1,0:T(8,128)(2,1)S(1)} %get-tuple-element.52), channel_id=1, source_target_pairs={{0,1},{1,0},{2,3},{3,2},{4,5},{5,4},{6,7},{7,6},{8,9},{9,8},{10,11... | collective-permute-start | bytes 393224 | tf_op jit(solution)/shard_map/ppermute | solution.py:373
